TPU v7x, 256 devices: a whole 4x4x8 slice. The times are simulated.
256 devices in a mesh: pb: 64 (over x, y, z_lo), col: 4 (over z_hi, core).
Axes of the slice: x: 4, y: 4, z: 8 (z_hi: 2, z_lo: 4; z = z_hi * 4 + z_lo), core: 2. Of those that a mesh axis runs over, the one named last changes fastest.
Arguments:
- vertex: bfloat16 [3, 256, 448, 896], P(None, 'pb', 'col'), may hold values from -6 to 6
- loop_blocks: bfloat16 [3, 256, 448, 896], P(None, ('pb', 'col')), may hold values from -0.013671875 to 0.013671875
- mixing: float32 [6, 256], replicated, may hold values from -1 to 1
- bond_offsets: int32 [7, 3], replicated, may hold values from -1 to 1
Outputs:
- new_vertex: bfloat16 [3, 256, 448, 896], P(None, 'pb', 'col')
All inputs are finite; a program needn't handle non-finite values.
Results may differ from a plain program's by a relative error of at most 0.007.
Values may be sent and summed in bfloat16 or wider, within the bound.
No kernel may reach another device: no remote copies, remote signals or barrier semaphores. Data moves between devices by JAX's collectives and lax.ppermute only.
A program may use at most 64 MiB of HBM per device.

v0:
```python
import math

import jax
import jax.numpy as jnp
from jax import lax
from jax.sharding import PartitionSpec as P

NB = 7
MX = 8


step_length = 0.25


def mesh_coords(momenta, mesh_y, mesh_z):
    flat_index = jnp.arange(momenta, dtype=jnp.int32)
    coord_x = flat_index // (mesh_y * mesh_z)
    coord_y = flat_index // mesh_z % mesh_y
    coord_z = flat_index % mesh_z
    return (coord_x, coord_y, coord_z)


def phase_tables(momenta, mesh_x, mesh_y, mesh_z):
    coord_x, coord_y, coord_z = mesh_coords(momenta, mesh_y, mesh_z)
    phase_index = (
        coord_x[:, None] * coord_x[None, :] * (mesh_y * mesh_z)
        + coord_y[:, None] * coord_y[None, :] * (mesh_x * mesh_z)
        + coord_z[:, None] * coord_z[None, :] * (mesh_x * mesh_y)
    ) % momenta
    angles = phase_index.astype(jnp.float32) * (2.0 * math.pi / momenta)
    cosine = jnp.cos(angles)
    sine_part = jnp.sin(angles)
    forward = jnp.stack([jnp.stack([cosine, sine_part], 1), jnp.stack([-sine_part, cosine], 1)]) * (
        1.0 / momenta
    )
    backward = jnp.stack([jnp.stack([cosine, -sine_part], 1), jnp.stack([sine_part, cosine], 1)])
    return (forward.astype(jnp.bfloat16), backward.astype(jnp.bfloat16))


def shifted_weights(mixing, bond_offsets, momenta, mesh_x, mesh_y, mesh_z):
    coord_x, coord_y, coord_z = mesh_coords(momenta, mesh_y, mesh_z)
    offsets = bond_offsets[:, None, :] - bond_offsets[None, :, :]
    shift_x = jnp.mod(coord_x[None, None, :] + offsets[:, :, 0:1], mesh_x)
    shift_y = jnp.mod(coord_y[None, None, :] + offsets[:, :, 1:2], mesh_y)
    shift_z = jnp.mod(coord_z[None, None, :] + offsets[:, :, 2:3], mesh_z)
    flat_slot = (shift_x * mesh_y + shift_y) * mesh_z + shift_z
    return jnp.take(mixing, flat_slot, axis=1)


def complex_batch(left_op, right_op):
    half_n = left_op.shape[1]
    real_part = jnp.einsum(
        "bij,bjk->bik", left_op[:, :, :half_n], right_op, preferred_element_type=jnp.float32
    )
    imag_part = jnp.einsum(
        "bij,bjk->bik", left_op[:, :, half_n:], right_op, preferred_element_type=jnp.float32
    )
    return jnp.concatenate(
        [
            real_part[:, :, :half_n] - imag_part[:, :, half_n:],
            real_part[:, :, half_n:] + imag_part[:, :, :half_n],
        ],
        axis=2,
    )


def per_device(vertex, loop_blocks, mixing, bond_offsets):
    groups = lax.axis_size("pb")
    mesh_z = vertex.shape[1]
    row_count = vertex.shape[2]
    full_order = vertex.shape[3] // 2
    narrow = full_order // groups
    momenta = mesh_z * groups
    mesh_y = groups // MX
    forward, backward = phase_tables(momenta, MX, mesh_y, mesh_z)
    weights = shifted_weights(mixing, bond_offsets, momenta, MX, mesh_y, mesh_z)
    split_cols = vertex.reshape(3, mesh_z, row_count, 2, full_order)
    gathered = lax.all_to_all(split_cols, "pb", split_axis=4, concat_axis=1, tiled=True)
    lattice = lax.dot_general(
        gathered, forward, (((3, 1), (0, 1)), ((), ())), preferred_element_type=jnp.float32
    )
    lattice = lax.optimization_barrier(lattice.astype(jnp.bfloat16)).astype(jnp.float32)
    blocks = lattice.reshape(3, row_count // NB, NB, narrow // NB, NB, 2, momenta)
    mixed_list = []
    for target in range(3):
        first_w = weights[2 * target][None, :, None, :, None, :]
        second_w = weights[2 * target + 1][None, :, None, :, None, :]
        summed = first_w * blocks[(target + 1) % 3] + second_w * blocks[(target + 2) % 3]
        mixed_list.append(summed.astype(jnp.bfloat16).reshape(row_count, narrow, 2, momenta))
    mixed_all = jnp.stack(mixed_list)
    projected = jnp.einsum(
        "tanpr,prsq->tqasn", mixed_all, backward, preferred_element_type=jnp.float32
    ).astype(jnp.bfloat16)
    returned_proj = lax.all_to_all(projected, "pb", split_axis=1, concat_axis=4, tiled=True)
    returned_proj = returned_proj.reshape(3, mesh_z, row_count, 2 * full_order)
    united_rows = (vertex.astype(jnp.float32) + returned_proj.astype(jnp.float32)).astype(
        jnp.bfloat16
    )
    united = lax.all_to_all(united_rows, "col", split_axis=1, concat_axis=2, tiled=True)
    local_q = united.shape[1]
    flat_united = united.reshape(3 * local_q, full_order, 2 * full_order)
    flat_loops = loop_blocks.reshape(3 * local_q, full_order, 2 * full_order)
    middle = complex_batch(flat_united, flat_loops).astype(jnp.bfloat16)
    change = complex_batch(middle, flat_united)
    increment = (
        (step_length * change).astype(jnp.bfloat16).reshape(3, local_q, full_order, 2 * full_order)
    )
    returned = lax.all_to_all(increment, "col", split_axis=2, concat_axis=1, tiled=True)
    return (vertex.astype(jnp.float32) + returned.astype(jnp.float32)).astype(jnp.bfloat16)


def solution(mesh):
    return jax.shard_map(
        per_device,
        mesh=mesh,
        in_specs=(P(None, "pb", "col", None), P(None, ("pb", "col"), None, None), P(), P()),
        out_specs=P(None, "pb", "col", None),
        check_vma=False,
    )
```

profile of v0, /device:TPU:1, one launch (start us, length us, event | category | flops | bytes accessed | tf_op | source)
XLA Modules:
  0.0 356.6 jit_solution(17212420372139971582)
XLA Ops:
  0.0 0.0 copy-start
  0.0 8.3 %reshape.772 = bf16[3,4,112,2,448]{4,3,2,1,0:T(2,128)(2,1)} reshape(bf16[3,4,112,896]{3,2,1,0:T(8,128)(2,1)} %param.4) | data formatting | bytes 4816896 | tf_op jit(solution)/shard_map/reshape | solution.py:77
  8.3 10.9 %copy.113 = bf16[3,4,112,2,448]{2,3,1,0,4:T(2,128)(2,1)} copy(bf16[3,4,112,2,448]{4,3,2,1,0:T(2,128)(2,1)} %reshape.772) | data formatting | bytes 4816896 | tf_op jit(solution)/shard_map/reshape | solution.py:77
  19.3 13.1 %all-to-all-start = ((bf16[3,4,112,2,448]{2,3,1,0,4:T(2,128)(2,1)}), bf16[3,4,112,2,448]{2,3,1,0,4:T(2,128)(2,1)}, u32[]{:S(2)}, u32[]{:S(2)}) async-start(bf16[3,4,112,2,448]{2,3,1,0,4:T(2,128)(2,1)} %copy.113), calls=%async_computation | async-start | bytes 5505024 | tf_op jit(solution)/shard_map/all_to_all | solution.py:78
  32.4 0.0 copy-start.14
  32.4 0.1 broadcast_subtract_fusion
  32.5 0.2 compare_select_fusion
  32.7 0.0 copy-done.16
  32.7 0.1 copy.109
  32.9 23.8 %gather_fusion = f32[12544,6]{1,0:T(8,128)} fusion(f32[6,256]{0,1:T(8,128)S(1)} %copy.109, s32[13312]{0:T(1024)S(1)} %pad_clamp_fusion), kind=kCustom, calls=%fused_computation | custom fusion | bytes 652288 | tf_op jit(solution)/shard_map/jit(_take)/gather | solution.py:47
  56.7 4.8 %copy.110 = f32[7,7,256,6]{2,1,0,3:T(8,128)S(1)} copy(f32[7,7,256,6]{3,2,1,0:T(8,128)} %bitcast.112) | data formatting | bytes 602112 | tf_op jit(solution)/shard_map/jit(_take)/gather | solution.py:47
  61.5 0.2 compare_and_fusion
  61.9 0.6 copy.118
  62.6 0.1 mul.481
  62.6 1.0 mul.482
  63.6 0.9 mul.486
  64.5 1.0 mul.487
  65.5 0.1 mul.491
  65.6 1.1 mul.492
  66.7 0.1 mul.496
  66.7 1.0 mul.497
  67.8 0.1 mul.501
  67.8 1.0 mul.502
  68.8 0.1 mul.474
  68.9 1.0 mul.475
  69.9 0.0 copy-done.15
  69.9 1.2 fusion.36
  71.1 0.9 maximum_bitcast_fusion.3
  72.0 0.1 maximum_bitcast_fusion.1
  72.1 24.1 %all-to-all-done = bf16[3,4,112,2,448]{2,3,1,0,4:T(2,128)(2,1)} async-done(((bf16[3,4,112,2,448]{2,3,1,0,4:T(2,128)(2,1)}), bf16[3,4,112,2,448]{2,3,1,0,4:T(2,128)(2,1)}, u32[]{:S(2)}, u32[]{:S(2)}) %all-to-all-start) | async-done | bytes 2408480 | tf_op jit(solution)/shard_map/all_to_all | solution.py:78
  96.2 3.0 copy.115
  99.2 1.5 fusion.8
  100.7 0.0 copy-start.2
  100.8 0.6 convert_element_type.113
  101.4 0.5 copy-done.2
  101.8 0.2 copy-done.3
  102.1 0.2 copy-done.4
  102.3 0.2 copy-done.5
  102.6 0.2 copy-done.6
  102.8 0.2 copy-done.7
  103.1 1.1 add_convert_fusion.2
  104.2 2.8 fusion.7
  107.0 8.6 %copy.124 = bf16[3,256,112,2,7]{2,3,4,0,1:T(2,128)(2,1)} copy(bf16[3,256,112,2,7]{1,2,4,0,3:T(8,128)(2,1)} %fusion.7) | data formatting | bytes 4816896 | tf_op jit(solution)/shard_map/convert_element_type | solution.py:93
  115.7 70.7 %all_to_all.45 = bf16[3,256,112,2,7]{2,3,4,0,1:T(2,128)(2,1)S(1)} all-to-all(bf16[3,256,112,2,7]{2,3,4,0,1:T(2,128)(2,1)} %copy.124), channel_id=1, replica_groups=mesh['pb'=64,'col'=4] {'pb'}, dimensions={1} | all-to-all | bytes 4816896 | tf_op jit(solution)/shard_map/all_to_all | solution.py:94
  186.3 0.6 copy.125
  187.0 0.7 convert_bitcast_fusion
  187.6 3.3 copy.126
  191.0 7.2 %copy.127 = f32[3,4,112,896]{3,2,1,0:T(8,128)} copy(f32[3,4,112,896]{2,1,3,0:T(4,128)} %bitcast.109) | data formatting | bytes 9633792 | tf_op jit(solution)/shard_map/convert_element_type | solution.py:96
  198.1 3.6 %fusion = bf16[3,4,112,896]{3,2,1,0:T(8,128)(2,1)S(1)} fusion(f32[3,4,112,896]{3,2,1,0:T(8,128)} %copy.127, bf16[3,4,112,896]{3,2,1,0:T(8,128)(2,1)} %param.4), kind=kLoop, calls=%fused_computation.4 | loop fusion | flops 3612672 | bytes 9633792 | tf_op jit(solution)/shard_map/convert_element_type | solution.py:96
  201.8 0.2 copy.128
  202.0 64.2 %all_to_all.46 = bf16[3,4,112,896]{3,2,0,1:T(8,128)(2,1)S(1)} all-to-all(bf16[3,4,112,896]{3,2,0,1:T(8,128)(2,1)S(1)} %copy.128), channel_id=1, replica_groups=mesh['pb'=64,'col'=4] {'col'}, dimensions={1} | all-to-all | bytes 4816896 | tf_op jit(solution)/shard_map/all_to_all | solution.py:99
  266.1 0.2 copy.129
  266.3 0.0 copy-done
  266.4 1.7 fusion.9
  268.0 1.6 fusion.11
  269.6 1.7 fusion.20
  271.3 1.7 fusion.18
  272.9 1.5 fusion.4
  274.4 0.9 fusion.2
  275.3 2.1 copy.130
  277.4 75.4 %all_to_all.47 = bf16[3,1,448,896]{3,0,1,2:T(4,128)(2,1)S(1)} all-to-all(bf16[3,1,448,896]{3,0,1,2:T(4,128)(2,1)S(1)} %copy.130), channel_id=1, replica_groups=mesh['pb'=64,'col'=4] {'col'}, dimensions={2} | all-to-all | bytes 4816896 | tf_op jit(solution)/shard_map/all_to_all | solution.py:108
  352.9 0.3 copy.131
  353.2 1.4 copy-done.1
  354.5 2.0 fusion.1
  (35 shorter events, 0.3 us)
Async XLA Ops:
  0.0 266.3 %copy-start = (bf16[3,1,448,896]{3,2,1,0:T(8,128)(2,1)S(1)}, bf16[3,1,448,896]{3,2,1,0:T(8,128)(2,1)}, u32[]{:S(2)}) copy-start(bf16[3,1,448,896]{3,2,1,0:T(8,128)(2,1)} %param.5) | copy-start | bytes 7225348
  19.3 13.1 %copy-start.17 = (s32[7,3]{0,1:T(4,128)S(1)}, s32[7,3]{0,1:T(4,128)}, u32[]{:S(2)}) copy-start(s32[7,3]{0,1:T(4,128)} %param.7) | copy-start | bytes 256
  19.3 13.4 %copy-start.16 = (f32[6,256]{1,0:T(8,128)S(1)}, f32[6,256]{1,0:T(8,128)}, u32[]{:S(2)}) copy-start(f32[6,256]{1,0:T(8,128)} %param.6) | copy-start | bytes 18436
  19.3 76.9 %all-to-all-start = ((bf16[3,4,112,2,448]{2,3,1,0,4:T(2,128)(2,1)}), bf16[3,4,112,2,448]{2,3,1,0,4:T(2,128)(2,1)}, u32[]{:S(2)}, u32[]{:S(2)}) async-start(bf16[3,4,112,2,448]{2,3,1,0,4:T(2,128)(2,1)} %copy.113), calls=%async_computation | async-start | bytes 5505024 | tf_op jit(solution)/shard_map/all_to_all | solution.py:78
  32.4 29.1 %copy-start.14 = (s32[256]{0:T(256)}, s32[256]{0:T(256)S(1)}, u32[]{:S(2)}) copy-start(s32[256]{0:T(256)S(1)} %and_select_fusion.3) | copy-start | bytes 3076
  32.4 29.1 %copy-start.10 = (s32[256]{0:T(256)}, s32[256]{0:T(256)S(1)}, u32[]{:S(2)}) copy-start(s32[256]{0:T(256)S(1)} %get-tuple-element.29) | copy-start | bytes 3076
  32.4 29.1 %copy-start.12 = (s32[256]{0:T(256)}, s32[256]{0:T(256)S(1)}, u32[]{:S(2)}) copy-start(s32[256]{0:T(256)S(1)} %get-tuple-element.30) | copy-start | bytes 3076
  67.8 2.2 copy-start.11
  67.8 2.2 copy-start.13
  67.8 2.2 copy-start.15
  100.7 1.1 copy-start.2
  100.7 1.4 copy-start.3
  100.7 1.6 copy-start.4
  100.7 1.8 copy-start.5
  100.7 2.1 copy-start.6
  100.8 2.3 copy-start.7
  103.1 1.1 copy-start.8
  103.1 1.1 copy-start.9
  352.9 1.7 copy-start.1
where the time goes:
time: 360 us; the launch traced here: 357 us
  blocking collectives  210 us (58%)
  local copies, waits for them, and re-layouts  84.8 us (24%)
  waiting for transfers between devices  24.1 us (7%)
  starting transfers between devices  13.1 us (4%)
  other arithmetic  13 us (4%)
  matrix products  10.9 us (3%)
    all_to_all x1, blocking collectives, per_device(): lax.all_to_all(increment, 'col', split_axis=2, concat_axis=1, tiled=True)  75.4 us
    all_to_all x1, blocking collectives, per_device(): lax.all_to_all(projected, 'pb', split_axis=1, concat_axis=4, tiled=True)  70.7 us
    all_to_all x1, blocking collectives, per_device(): lax.all_to_all(united_rows, 'col', split_axis=1, concat_axis=2, tiled=True)  64.2 us
    gather x2, local copies, waits for them, and re-layouts, shifted_weights(): return jnp.take(mixing, flat_slot, axis=1)  28.6 us
    all_to_all x1, waiting for transfers between devices, per_device(): lax.all_to_all(split_cols, 'pb', split_axis=4, concat_axis=1, tiled=True)  24.1 us
    reshape x2, local copies, waits for them, and re-layouts, per_device(): split_cols = vertex.reshape(3, mesh_z, row_count, 2, full_order)  19.3 us
    all_to_all x1, starting transfers between devices, per_device(): lax.all_to_all(split_cols, 'pb', split_axis=4, concat_axis=1, tiled=True)  13.1 us
    convert_element_type x2, local copies, waits for them, and re-layouts, per_device(): returned_proj.astype(jnp.float32)  10.5 us
  transfers between devices with their start and end apart: 1, of which 1 were waited for; matrix products, arithmetic and copies ran while one was open for 11% of the time, Pallas kernels for 0%

commit v1 on v0

v1 whole, which is shorter than its diff:
```python
import math

import jax
import jax.numpy as jnp
from jax import lax
from jax.sharding import PartitionSpec as P

NB = 7
MX = 8


step_length = 0.25


def mesh_coords(momenta, mesh_y, mesh_z):
    flat_index = jnp.arange(momenta, dtype=jnp.int32)
    coord_x = flat_index // (mesh_y * mesh_z)
    coord_y = flat_index // mesh_z % mesh_y
    coord_z = flat_index % mesh_z
    return (coord_x, coord_y, coord_z)


def phase_tables(momenta, mesh_x, mesh_y, mesh_z):
    coord_x, coord_y, coord_z = mesh_coords(momenta, mesh_y, mesh_z)
    phase_index = (
        coord_x[:, None] * coord_x[None, :] * (mesh_y * mesh_z)
        + coord_y[:, None] * coord_y[None, :] * (mesh_x * mesh_z)
        + coord_z[:, None] * coord_z[None, :] * (mesh_x * mesh_y)
    ) % momenta
    angles = phase_index.astype(jnp.float32) * (2.0 * math.pi / momenta)
    cosine = jnp.cos(angles)
    sine_part = jnp.sin(angles)
    forward = jnp.stack([jnp.stack([cosine, sine_part], 1), jnp.stack([-sine_part, cosine], 1)]) * (
        1.0 / momenta
    )
    backward = jnp.stack([jnp.stack([cosine, -sine_part], 1), jnp.stack([sine_part, cosine], 1)])
    return (forward.astype(jnp.bfloat16), backward.astype(jnp.bfloat16))


def shifted_weights(mixing, bond_offsets, momenta, mesh_x, mesh_y, mesh_z):
    coord_x, coord_y, coord_z = mesh_coords(momenta, mesh_y, mesh_z)
    offsets = bond_offsets[:, None, :] - bond_offsets[None, :, :]
    shift_x = jnp.mod(coord_x[None, None, :] + offsets[:, :, 0:1], mesh_x)
    shift_y = jnp.mod(coord_y[None, None, :] + offsets[:, :, 1:2], mesh_y)
    shift_z = jnp.mod(coord_z[None, None, :] + offsets[:, :, 2:3], mesh_z)
    flat_slot = (shift_x * mesh_y + shift_y) * mesh_z + shift_z
    return jnp.take(mixing, flat_slot, axis=1)


def per_device(vertex, loop_blocks, mixing, bond_offsets):
    groups = lax.axis_size("pb")
    cols = lax.axis_size("col")
    mesh_z = vertex.shape[1]
    row_count = vertex.shape[2]
    order = vertex.shape[3] // 2
    narrow = order // groups
    momenta = mesh_z * groups
    mesh_y = groups // MX
    forward, backward = phase_tables(momenta, MX, mesh_y, mesh_z)
    weights = shifted_weights(mixing, bond_offsets, momenta, MX, mesh_y, mesh_z)
    split = vertex.reshape(3, mesh_z, row_count, 2, groups, narrow).transpose(4, 1, 3, 0, 5, 2)
    gathered = lax.all_to_all(split, "pb", split_axis=0, concat_axis=0, tiled=True)
    x = gathered.reshape(momenta, 2, 3, narrow, row_count)
    lattice = jnp.einsum("qptna,pqsr->rstna", x, forward, preferred_element_type=jnp.float32)
    lattice = lax.optimization_barrier(lattice.astype(jnp.bfloat16)).astype(jnp.float32)
    w = jnp.tile(weights.transpose(0, 3, 2, 1), (1, 1, 1, row_count // NB))
    mixed = []
    for t in range(3):
        summed = (
            w[2 * t][:, None] * lattice[:, :, (t + 1) % 3]
            + w[2 * t + 1][:, None] * lattice[:, :, (t + 2) % 3]
        )
        mixed.append(summed.astype(jnp.bfloat16))
    mixed = jnp.stack(mixed, axis=2)
    projected = jnp.einsum(
        "rptna,prsq->qstna", mixed, backward, preferred_element_type=jnp.float32
    ).astype(jnp.bfloat16)
    united = (x.astype(jnp.float32) + projected.astype(jnp.float32)).astype(jnp.bfloat16)
    sent = lax.all_to_all(united, ("pb", "col"), split_axis=0, concat_axis=0, tiled=True)
    ut = sent.reshape(groups, cols, 2, 3, narrow, row_count).transpose(3, 2, 0, 4, 1, 5)
    ut = ut.reshape(3, 2, order, order)
    u = ut.transpose(0, 3, 1, 2)
    loops = loop_blocks.reshape(3, order, 2 * order)
    outs = []
    for t in range(3):
        ur, ui = ut[t, 0], ut[t, 1]
        f = lambda l, r: jnp.einsum("ca,cd->ad", l, r, preferred_element_type=jnp.float32)
        re, im = f(ur, loops[t]), f(ui, loops[t])
        m_re = (re[:, :order] - im[:, order:]).astype(jnp.bfloat16)
        m_im = (re[:, order:] + im[:, :order]).astype(jnp.bfloat16)
        g = lambda l, r: jnp.einsum("ad,cd->ac", l, r, preferred_element_type=jnp.float32)
        c_re = g(m_re, ur) - g(m_im, ui)
        c_im = g(m_re, ui) + g(m_im, ur)
        outs.append((step_length * jnp.concatenate([c_re, c_im], axis=1)).astype(jnp.bfloat16))
    increment = jnp.stack(outs, axis=1).reshape(cols, row_count, 3, 2 * order)
    increment = jnp.stack(outs).reshape(3, cols, row_count, 2 * order).transpose(1, 0, 2, 3)
    returned = lax.all_to_all(increment, "col", split_axis=0, concat_axis=0, tiled=True)
    returned = returned.transpose(1, 0, 2, 3)
    return (vertex.astype(jnp.float32) + returned.astype(jnp.float32)).astype(jnp.bfloat16)


def solution(mesh):
    return jax.shard_map(
        per_device,
        mesh=mesh,
        in_specs=(P(None, "pb", "col", None), P(None, ("pb", "col"), None, None), P(), P()),
        out_specs=P(None, "pb", "col", None),
        check_vma=False,
    )
```

time: 360 us -> 272 us (0.76)
  blocking collectives: 210 us -> 139 us
  waiting for transfers between devices: 24.1 us -> 7.38 us
  matrix products: 10.9 us -> 15.6 us
    all_to_all x3 -> x2, blocking collectives: 210 us -> 139 us  [the longest x1 78.3 us: per_device(): lax.all_to_all(united, ('pb', 'col'), split_axis=0, concat_axis=0, tiled=...]
    another operation x0 -> x12, local copies, waits for them, and re-layouts: none -> 22.3 us  [per_device(): w = jnp.tile(weights.transpose(0, 3, 2, 1), (1, 1, 1, row_count // NB))]
    all_to_all x1, waiting for transfers between devices: 24.1 us -> 7.38 us  [per_device(): lax.all_to_all(split, 'pb', split_axis=0, concat_axis=0, tiled=True)]
    convert_element_type x5 -> x2, local copies, waits for them, and re-layouts: 21.4 us -> 9.09 us  [the longest x1 7.47 us: per_device(): (x.astype(jnp.float32) + projected.astype(jnp.float32)).astype(jnp.bfloat16)]
    reshape x2, local copies, waits for them, and re-layouts: 19.3 us -> 9.19 us  [the longest x1 4.61 us: per_device(): ut = ut.reshape(3, 2, order, order)]
    mul x19 -> x0, local copies, waits for them, and re-layouts: 8.06 us -> none  [the longest x10 4.76 us: per_device(): first_w * blocks[(target + 1) % 3] + second_w * blocks[(target + 2) % 3]]
    transpose x0 -> x2, local copies, waits for them, and re-layouts: none -> 4.96 us  [the longest x1 2.48 us: per_device(): sent.reshape(groups, cols, 2, 3, narrow, row_count)]
    dot_general x6 -> x20, matrix products: 10.9 us -> 15.6 us  [the longest x6 5.25 us: per_device(): jnp.einsum('ca,cd->ad', l, r, preferred_element_type=jnp.float32)]
  transfers between devices with their start and end apart: 1 -> 1, of which waited for: 1 -> 1; matrix products, arithmetic and copies ran while one was open for 11% -> 21% of each run, Pallas kernels for 0% -> 0%
where the time goes in v1:
time: 272 us; the launch traced here: 271 us
  blocking collectives  139 us (51%)
  local copies, waits for them, and re-layouts  86.3 us (32%)
  matrix products  15.6 us (6%)
  starting transfers between devices  12.7 us (5%)
  other arithmetic  9.72 us (4%)
  waiting for transfers between devices  7.38 us (3%)
    all_to_all x1, blocking collectives, per_device(): lax.all_to_all(united, ('pb', 'col'), split_axis=0, concat_axis=0, tiled=...  78.3 us
    all_to_all x1, blocking collectives, per_device(): lax.all_to_all(increment, 'col', split_axis=0, concat_axis=0, tiled=True)  60.5 us
    gather x2, local copies, waits for them, and re-layouts, shifted_weights(): return jnp.take(mixing, flat_slot, axis=1)  28.8 us
    another operation x12, local copies, waits for them, and re-layouts, per_device(): w = jnp.tile(weights.transpose(0, 3, 2, 1), (1, 1, 1, row_count // NB))  22.3 us
    all_to_all x1, starting transfers between devices, per_device(): lax.all_to_all(split, 'pb', split_axis=0, concat_axis=0, tiled=True)  12.7 us
    convert_element_type x1, local copies, waits for them, and re-layouts, per_device(): (x.astype(jnp.float32) + projected.astype(jnp.float32)).astype(jnp.bfloat16)  7.47 us
    all_to_all x1, waiting for transfers between devices, per_device(): lax.all_to_all(split, 'pb', split_axis=0, concat_axis=0, tiled=True)  7.38 us
    unnamed x34, local copies, waits for them, and re-layouts  7.29 us
  transfers between devices with their start and end apart: 1, of which 1 were waited for; matrix products, arithmetic and copies ran while one was open for 21% of the time, Pallas kernels for 0%

profile of v1, /device:TPU:1, one launch (start us, length us, event | category | flops | bytes accessed | tf_op | source)
XLA Modules:
  0.0 271.0 jit_solution(9244419416378173148)
XLA Ops:
  0.0 5.0 %copy.56 = bf16[3,4,112,896]{2,1,3,0:T(4,128)(2,1)S(1)} copy(bf16[3,4,112,896]{3,2,1,0:T(8,128)(2,1)} %param.4) | data formatting | bytes 4816896 | tf_op args[0]
  5.0 2.5 copy.57
  7.5 12.7 %all-to-all-start = ((bf16[64,4,2,3,7,112]{5,1,4,2,3,0:T(4,128)(2,1)}), bf16[64,4,2,3,7,112]{5,1,4,2,3,0:T(4,128)(2,1)S(1)}, u32[]{:S(2)}, u32[]{:S(2)}) async-start(bf16[64,4,2,3,7,112]{5,1,4,2,3,0:T(4,128)(2,1)} %copy.57), calls=%async_computation | async-start | bytes 5505024 | tf_op jit(solution)/shard_map/all_to_all | solution.py:62
  20.7 24.0 %gather_fusion = f32[12544,6]{1,0:T(8,128)} fusion(f32[6,256]{0,1:T(8,128)S(1)} %copy.63, s32[13312]{0:T(1024)S(1)} %pad_clamp_fusion), kind=kCustom, calls=%fused_computation | custom fusion | bytes 652288 | tf_op jit(solution)/shard_map/jit(_take)/gather | solution.py:47
  44.7 4.8 %copy.64 = f32[7,7,256,6]{2,0,1,3:T(8,128)S(1)} copy(f32[7,7,256,6]{3,2,1,0:T(8,128)} %bitcast.183) | data formatting | bytes 602112 | tf_op jit(solution)/shard_map/jit(_take)/gather | solution.py:47
  50.0 0.7 slice_bitcast_fusion.29
  50.7 1.0 tile.31
  51.7 1.3 tile.32
  53.0 1.8 tile.29
  54.8 2.2 tile.30
  57.0 1.8 tile.35
  58.8 2.2 tile.36
  61.0 1.8 tile.33
  62.8 2.2 tile.34
  65.0 1.8 tile.39
  66.8 2.2 tile.40
  69.0 1.8 tile.37
  70.8 2.2 tile.38
  73.0 1.9 fusion.53
  75.0 0.8 maximum_bitcast_fusion.4
  75.8 1.2 maximum_bitcast_fusion.2
  77.0 7.4 %all-to-all-done = bf16[64,4,2,3,7,112]{5,1,4,2,3,0:T(4,128)(2,1)S(1)} async-done(((bf16[64,4,2,3,7,112]{5,1,4,2,3,0:T(4,128)(2,1)}), bf16[64,4,2,3,7,112]{5,1,4,2,3,0:T(4,128)(2,1)S(1)}, u32[]{:S(2)}, u32[]{:S(2)}) %all-to-all-start) | async-done | bytes 2408480 | tf_op jit(solution)/shard_map/all_to_all | solution.py:62
  84.3 3.0 %copy.58 = bf16[64,4,2,3,7,112]{5,1,0,4,3,2:T(4,128)(2,1)} copy(bf16[64,4,2,3,7,112]{5,1,4,2,3,0:T(4,128)(2,1)S(1)} %all-to-all-done) | data formatting | bytes 4816896 | tf_op jit(solution)/shard_map/all_to_all | solution.py:62
  87.4 4.6 %copy.59 = bf16[256,2,3,7,112]{0,4,3,2,1:T(8,128)(2,1)} copy(bf16[256,2,3,7,112]{4,0,3,2,1:T(8,128)(2,1)} %bitcast.179) | data formatting | bytes 4816896 | tf_op jit(solution)/shard_map/reshape | solution.py:63
  91.9 2.6 fusion.2
  94.6 0.6 convert_element_type.142
  95.3 0.5 copy-done.3
  96.0 0.2 copy-done.5
  96.7 1.1 add_convert_fusion.2
  97.8 0.6 copy-done.8
  98.5 2.6 fusion.1
  101.1 7.5 %copy.69 = bf16[256,2,3,7,112]{4,1,3,2,0:T(2,128)(2,1)S(1)} copy(bf16[256,2,3,7,112]{0,4,3,2,1:T(8,128)(2,1)} %fusion.1) | data formatting | bytes 4816896 | tf_op jit(solution)/shard_map/convert_element_type | solution.py:78
  108.6 78.3 %all_to_all.15 = bf16[256,2,3,7,112]{4,1,3,2,0:T(2,128)(2,1)S(1)} all-to-all(bf16[256,2,3,7,112]{4,1,3,2,0:T(2,128)(2,1)S(1)} %copy.69), channel_id=1, replica_groups=mesh['pb'=64,'col'=4] {'pb','col'}, dimensions={0} | all-to-all | bytes 4816896 | tf_op jit(solution)/shard_map/all_to_all | solution.py:79
  186.8 0.7 copy.70
  187.5 2.5 copy.71
  190.0 4.6 %reshape.827 = bf16[3,2,448,448]{3,2,1,0:T(8,128)(2,1)S(1)} reshape(bf16[3,2,64,7,4,112]{5,4,3,2,1,0:T(4,128)(2,1)} %copy.71) | data formatting | bytes 4816896 | tf_op jit(solution)/shard_map/reshape | solution.py:81
  194.6 1.9 fusion.18
  196.6 0.7 fusion.20
  197.3 0.6 fusion.12
  197.8 0.4 fusion.45
  198.3 0.4 fusion.44
  198.7 0.7 fusion.22
  199.4 0.7 fusion.24
  200.0 0.6 fusion.14
  200.6 0.4 fusion.43
  201.0 0.4 fusion.42
  201.5 0.7 fusion.26
  202.1 0.7 fusion.28
  202.8 0.6 fusion.16
  203.4 0.4 fusion.41
  203.8 0.4 fusion.40
  204.2 0.4 convolution_add_fusion
  204.7 0.4 convolution_subtract_fusion
  205.1 0.4 convolution_add_fusion.1
  205.5 0.4 convolution_subtract_fusion.1
  206.0 0.4 convolution_add_fusion.2
  206.4 0.4 convolution_subtract_fusion.2
  206.8 0.3 fusion.10
  207.1 0.3 fusion.9
  207.5 0.3 fusion.8
  207.8 0.3 maximum_bitcast_fusion
  208.1 60.5 %all_to_all.16 = bf16[4,3,112,896]{3,2,1,0:T(8,128)(2,1)S(1)} all-to-all(bf16[4,3,112,896]{3,2,1,0:T(8,128)(2,1)S(1)} %maximum_bitcast_fusion), channel_id=1, replica_groups=mesh['pb'=64,'col'=4] {'col'}, dimensions={0} | all-to-all | bytes 4816896 | tf_op jit(solution)/shard_map/all_to_all | solution.py:97
  268.7 0.7 fusion
  269.3 1.6 copy.78
  (42 shorter events, 1.7 us)
Async XLA Ops:
  7.5 12.7 %copy-start.14 = (f32[6,256]{1,0:T(8,128)S(1)}, f32[6,256]{1,0:T(8,128)}, u32[]{:S(2)}) copy-start(f32[6,256]{1,0:T(8,128)} %param.6) | copy-start | bytes 18436
  7.5 12.9 %copy-start.15 = (s32[7,3]{0,1:T(4,128)S(1)}, s32[7,3]{0,1:T(4,128)}, u32[]{:S(2)}) copy-start(s32[7,3]{0,1:T(4,128)} %param.7) | copy-start | bytes 256
  7.5 76.8 %all-to-all-start = ((bf16[64,4,2,3,7,112]{5,1,4,2,3,0:T(4,128)(2,1)}), bf16[64,4,2,3,7,112]{5,1,4,2,3,0:T(4,128)(2,1)S(1)}, u32[]{:S(2)}, u32[]{:S(2)}) async-start(bf16[64,4,2,3,7,112]{5,1,4,2,3,0:T(4,128)(2,1)} %copy.57), calls=%async_computation | async-start | bytes 5505024 | tf_op jit(solution)/shard_map/all_to_all | solution.py:62
  20.4 29.4 %copy-start.13 = (s32[256]{0:T(256)}, s32[256]{0:T(256)S(1)}, u32[]{:S(2)}) copy-start(s32[256]{0:T(256)S(1)} %and_select_fusion.3) | copy-start | bytes 3076
  20.4 29.4 %copy-start.11 = (s32[256]{0:T(256)}, s32[256]{0:T(256)S(1)}, u32[]{:S(2)}) copy-start(s32[256]{0:T(256)S(1)} %get-tuple-element.36) | copy-start | bytes 3076
  20.4 29.4 %copy-start.12 = (s32[256]{0:T(256)}, s32[256]{0:T(256)S(1)}, u32[]{:S(2)}) copy-start(s32[256]{0:T(256)S(1)} %get-tuple-element.37) | copy-start | bytes 3076
  87.3 4.6 %copy-start = (bf16[64,4,2,3,7,112]{5,1,0,4,3,2:T(4,128)(2,1)S(1)}, bf16[64,4,2,3,7,112]{5,1,0,4,3,2:T(4,128)(2,1)}, u32[]{:S(2)}) copy-start(bf16[64,4,2,3,7,112]{5,1,0,4,3,2:T(4,128)(2,1)} %copy.58) | copy-start | bytes 7225348
  94.6 1.1 copy-start.3
  94.6 1.4 copy-start.4
  94.6 1.6 copy-start.5
  94.6 1.8 copy-start.6
  94.6 2.1 copy-start.7
  96.7 1.7 copy-start.8
  96.7 1.7 copy-start.9
  96.7 1.7 copy-start.10
  194.6 2.0 copy-start.2
  208.1 60.6 %copy-start.1 = (bf16[3,4,112,896]{3,2,1,0:T(8,128)(2,1)S(1)}, bf16[3,4,112,896]{3,2,1,0:T(8,128)(2,1)}, u32[]{:S(2)}) copy-start(bf16[3,4,112,896]{3,2,1,0:T(8,128)(2,1)} %param.4) | copy-start | bytes 7225348

commit v2 on v1

--- a/solution.py
+++ b/solution.py
@@ -81,22 +81,38 @@
     ut = ut.reshape(3, 2, order, order)
     u = ut.transpose(0, 3, 1, 2)
     loops = loop_blocks.reshape(3, order, 2 * order)
+    mine = lax.axis_index("col")
     outs = []
     for t in range(3):
-        ur, ui = ut[t, 0], ut[t, 1]
+        ur, ui, loop = ut[t, 0], ut[t, 1], loops[t]
+        if t:
+            ur, ui, loop, increment = lax.optimization_barrier((ur, ui, loop, increment))
         f = lambda l, r: jnp.einsum("ca,cd->ad", l, r, preferred_element_type=jnp.float32)
-        re, im = f(ur, loops[t]), f(ui, loops[t])
+        re, im = f(ur, loop), f(ui, loop)
         m_re = (re[:, :order] - im[:, order:]).astype(jnp.bfloat16)
         m_im = (re[:, order:] + im[:, :order]).astype(jnp.bfloat16)
         g = lambda l, r: jnp.einsum("ad,cd->ac", l, r, preferred_element_type=jnp.float32)
         c_re = g(m_re, ur) - g(m_im, ui)
         c_im = g(m_re, ui) + g(m_im, ur)
-        outs.append((step_length * jnp.concatenate([c_re, c_im], axis=1)).astype(jnp.bfloat16))
-    increment = jnp.stack(outs, axis=1).reshape(cols, row_count, 3, 2 * order)
-    increment = jnp.stack(outs).reshape(3, cols, row_count, 2 * order).transpose(1, 0, 2, 3)
-    returned = lax.all_to_all(increment, "col", split_axis=0, concat_axis=0, tiled=True)
-    returned = returned.transpose(1, 0, 2, 3)
-    return (vertex.astype(jnp.float32) + returned.astype(jnp.float32)).astype(jnp.bfloat16)
+        increment = (step_length * jnp.concatenate([c_re, c_im], axis=1)).astype(jnp.bfloat16)
+        increment = increment.reshape(cols, row_count, 2 * order)
+        pieces = []
+        for k in range(cols):
+            piece = lax.dynamic_index_in_dim(increment, mine ^ k, 0, keepdims=False)
+            if k:
+                piece = lax.ppermute(piece, "col", [(i, i ^ k) for i in range(cols)])
+            pieces.append(piece)
+        low, high = (mine & 1) == 1, (mine & 2) == 2
+        a, b, c, d = pieces
+        a, b = jnp.where(low, b, a), jnp.where(low, a, b)
+        c, d = jnp.where(low, d, c), jnp.where(low, c, d)
+        a, c = jnp.where(high, c, a), jnp.where(high, a, c)
+        b, d = jnp.where(high, d, b), jnp.where(high, b, d)
+        returned = jnp.stack([a, b, c, d])
+        outs.append(
+            (vertex[t].astype(jnp.float32) + returned.astype(jnp.float32)).astype(jnp.bfloat16)
+        )
+    return jnp.stack(outs)
 
 
 def solution(mesh):

time: 272 us -> 269 us (0.989)
  blocking collectives: 139 us -> 0 us
  waiting for transfers between devices: 7.38 us -> 109 us
  starting transfers between devices: 12.7 us -> 44.7 us
    all_to_all x2 -> x0, blocking collectives: 139 us -> none  [the longest x1 78.3 us: per_device(): lax.all_to_all(united, ('pb', 'col'), split_axis=0, concat_axis=0, tiled=...]
    all_to_all x0 -> x1, waiting for transfers between devices: none -> 66.3 us  [per_device(): lax.all_to_all(united, ('pb', 'col'), split_axis=0, concat_axis=0, tiled=...]
    ppermute x0 -> x9, waiting for transfers between devices: none -> 35.3 us  [per_device(): piece = lax.ppermute(piece, 'col', [(i, i ^ k) for i in range(cols)])]
    ppermute x0 -> x9, starting transfers between devices: none -> 22.3 us  [per_device(): piece = lax.ppermute(piece, 'col', [(i, i ^ k) for i in range(cols)])]
    all_to_all x0 -> x1, starting transfers between devices: none -> 9.74 us  [per_device(): lax.all_to_all(united, ('pb', 'col'), split_axis=0, concat_axis=0, tiled=...]
  transfers between devices with their start and end apart: 1 -> 11, of which waited for: 1 -> 8; matrix products, arithmetic and copies ran while one was open for 21% -> 23% of each run, Pallas kernels for 0% -> 0%
where the time goes in v2:
time: 269 us; the launch traced here: 268 us
  waiting for transfers between devices  109 us (41%)
  local copies, waits for them, and re-layouts  86.9 us (32%)
  starting transfers between devices  44.7 us (17%)
  matrix products  15.7 us (6%)
  other arithmetic  11.5 us (4%)
    all_to_all x1, waiting for transfers between devices, per_device(): lax.all_to_all(united, ('pb', 'col'), split_axis=0, concat_axis=0, tiled=...  66.3 us
    ppermute x9, waiting for transfers between devices, per_device(): piece = lax.ppermute(piece, 'col', [(i, i ^ k) for i in range(cols)])  35.3 us
    gather x2, local copies, waits for them, and re-layouts, shifted_weights(): return jnp.take(mixing, flat_slot, axis=1)  28.8 us
    ppermute x9, starting transfers between devices, per_device(): piece = lax.ppermute(piece, 'col', [(i, i ^ k) for i in range(cols)])  22.3 us
    another operation x12, local copies, waits for them, and re-layouts, per_device(): w = jnp.tile(weights.transpose(0, 3, 2, 1), (1, 1, 1, row_count // NB))  22.3 us
    all_to_all x1, starting transfers between devices, per_device(): lax.all_to_all(split, 'pb', split_axis=0, concat_axis=0, tiled=True)  12.7 us
    all_to_all x1, starting transfers between devices, per_device(): lax.all_to_all(united, ('pb', 'col'), split_axis=0, concat_axis=0, tiled=...  9.74 us
    unnamed x34, local copies, waits for them, and re-layouts  7.66 us
  transfers between devices with their start and end apart: 11, of which 8 were waited for; matrix products, arithmetic and copies ran while one was open for 23% of the time, Pallas kernels for 0%

profile of v2, /device:TPU:1, one launch (start us, length us, event | category | flops | bytes accessed | tf_op | source)
XLA Modules:
  0.0 268.3 jit_solution(13763234789137706811)
XLA Ops:
  0.0 5.0 %copy.47 = bf16[3,4,112,896]{2,1,3,0:T(4,128)(2,1)S(1)} copy(bf16[3,4,112,896]{3,2,1,0:T(8,128)(2,1)} %param.4) | data formatting | bytes 4816896 | tf_op args[0]
  5.0 2.5 copy.48
  7.5 12.7 %all-to-all-start = ((bf16[64,4,2,3,7,112]{5,1,4,2,3,0:T(4,128)(2,1)}), bf16[64,4,2,3,7,112]{5,1,4,2,3,0:T(4,128)(2,1)S(1)}, u32[]{:S(2)}, u32[]{:S(2)}) async-start(bf16[64,4,2,3,7,112]{5,1,4,2,3,0:T(4,128)(2,1)} %copy.48), calls=%async_computation | async-start | bytes 5505024 | tf_op jit(solution)/shard_map/all_to_all | solution.py:62
  20.7 23.9 %gather_fusion = f32[12544,6]{1,0:T(8,128)} fusion(f32[6,256]{0,1:T(8,128)S(1)} %copy.54, s32[13312]{0:T(1024)S(1)} %pad_clamp_fusion), kind=kCustom, calls=%fused_computation | custom fusion | bytes 652288 | tf_op jit(solution)/shard_map/jit(_take)/gather | solution.py:47
  44.6 4.8 %copy.55 = f32[7,7,256,6]{2,0,1,3:T(8,128)S(1)} copy(f32[7,7,256,6]{3,2,1,0:T(8,128)} %bitcast.238) | data formatting | bytes 602112 | tf_op jit(solution)/shard_map/jit(_take)/gather | solution.py:47
  50.0 0.7 slice_bitcast_fusion.19
  50.7 1.0 tile.31
  51.7 1.3 tile.32
  53.0 1.8 tile.29
  54.8 2.2 tile.30
  57.0 1.8 tile.35
  58.8 2.2 tile.36
  61.0 1.8 tile.33
  62.8 2.2 tile.34
  65.0 1.8 tile.39
  66.8 2.2 tile.40
  69.0 1.8 tile.37
  70.8 2.2 tile.38
  73.0 1.9 fusion.36
  75.0 0.8 maximum_bitcast_fusion.3
  75.8 1.1 maximum_bitcast_fusion.1
  76.9 7.4 %all-to-all-done = bf16[64,4,2,3,7,112]{5,1,4,2,3,0:T(4,128)(2,1)S(1)} async-done(((bf16[64,4,2,3,7,112]{5,1,4,2,3,0:T(4,128)(2,1)}), bf16[64,4,2,3,7,112]{5,1,4,2,3,0:T(4,128)(2,1)S(1)}, u32[]{:S(2)}, u32[]{:S(2)}) %all-to-all-start) | async-done | bytes 2408480 | tf_op jit(solution)/shard_map/all_to_all | solution.py:62
  84.3 3.0 %copy.49 = bf16[64,4,2,3,7,112]{5,1,0,4,3,2:T(4,128)(2,1)} copy(bf16[64,4,2,3,7,112]{5,1,4,2,3,0:T(4,128)(2,1)S(1)} %all-to-all-done) | data formatting | bytes 4816896 | tf_op jit(solution)/shard_map/all_to_all | solution.py:62
  87.3 4.6 %copy.50 = bf16[256,2,3,7,112]{0,4,3,2,1:T(8,128)(2,1)} copy(bf16[256,2,3,7,112]{4,0,3,2,1:T(8,128)(2,1)} %bitcast.234) | data formatting | bytes 4816896 | tf_op jit(solution)/shard_map/reshape | solution.py:63
  91.9 2.7 fusion.1
  94.6 0.6 convert_element_type.163
  95.2 0.5 copy-done.3
  96.7 1.1 add_convert_fusion.5
  97.8 0.6 copy-done.8
  98.4 1.6 fusion
  100.1 6.6 %copy.60 = bf16[256,2,3,7,112]{4,1,3,2,0:T(2,128)(2,1)} copy(bf16[256,2,3,7,112]{0,4,3,2,1:T(8,128)(2,1)S(1)} %fusion) | data formatting | bytes 4816896 | tf_op jit(solution)/shard_map/convert_element_type | solution.py:78
  106.6 9.7 %all-to-all-start.1 = ((bf16[256,2,3,7,112]{4,1,3,2,0:T(2,128)(2,1)}), bf16[256,2,3,7,112]{4,1,3,2,0:T(2,128)(2,1)S(1)}, u32[]{:S(2)}, u32[]{:S(2)}) async-start(bf16[256,2,3,7,112]{4,1,3,2,0:T(2,128)(2,1)} %copy.60), calls=%async_computation.1 | async-start | bytes 5505024 | tf_op jit(solution)/shard_map/all_to_all | solution.py:79
  116.4 2.4 slice_bitcast_fusion.1
  118.8 66.3 %all-to-all-done.1 = bf16[256,2,3,7,112]{4,1,3,2,0:T(2,128)(2,1)S(1)} async-done(((bf16[256,2,3,7,112]{4,1,3,2,0:T(2,128)(2,1)}), bf16[256,2,3,7,112]{4,1,3,2,0:T(2,128)(2,1)S(1)}, u32[]{:S(2)}, u32[]{:S(2)}) %all-to-all-start.1) | async-done | bytes 2408480 | tf_op jit(solution)/shard_map/all_to_all | solution.py:79
  185.1 0.7 copy.61
  185.8 2.5 copy.62
  188.3 4.6 %reshape.901 = bf16[3,2,448,448]{3,2,1,0:T(8,128)(2,1)S(1)} reshape(bf16[3,2,64,7,4,112]{5,4,3,2,1,0:T(4,128)(2,1)} %copy.62) | data formatting | bytes 4816896 | tf_op jit(solution)/shard_map/reshape | solution.py:81
  192.9 1.8 fusion.17
  194.7 1.8 fusion.19
  196.5 0.6 fusion.15
  198.1 0.4 convolution_add_fusion.2
  199.6 0.7 fusion.58
  200.3 0.7 fusion.57
  201.0 0.6 fusion.13
  202.9 0.4 convolution_subtract_fusion.1
  203.6 0.7 fusion.62
  204.3 0.7 fusion.61
  205.0 0.6 fusion.11
  206.5 1.4 collective-permute-start
  207.8 5.0 %collective-permute-start.1 = (bf16[112,896]{1,0:T(8,128)(2,1)S(1)}, bf16[112,896]{1,0:T(8,128)(2,1)S(1)}, u32[]{:S(2)}, u32[]{:S(2)}) collective-permute-start(bf16[112,896]{1,0:T(8,128)(2,1)S(1)} %get-tuple-element.48), channel_id=1, source_target_pairs={{0,2},{1,3},{2,0},{3,1},{4,6},{5,7},{6,4},{7,5},{8,10},{9,11},{10,... | collective-permute-start | bytes 602120 | tf_op jit(solution)/shard_map/ppermute | solution.py:103
  214.1 0.8 collective-permute-start.6
  215.0 5.0 %collective-permute-start.7 = (bf16[112,896]{1,0:T(8,128)(2,1)S(1)}, bf16[112,896]{1,0:T(8,128)(2,1)S(1)}, u32[]{:S(2)}, u32[]{:S(2)}) collective-permute-start(bf16[112,896]{1,0:T(8,128)(2,1)S(1)} %get-tuple-element.54), channel_id=1, source_target_pairs={{0,2},{1,3},{2,0},{3,1},{4,6},{5,7},{6,4},{7,5},{8,10},{9,11},{10,... | collective-permute-start | bytes 602120 | tf_op jit(solution)/shard_map/ppermute | solution.py:103
  220.0 1.0 collective-permute-done
  221.0 0.7 collective-permute-start.8
  221.7 9.2 %collective-permute-done.1 = bf16[112,896]{1,0:T(8,128)(2,1)S(1)} collective-permute-done((bf16[112,896]{1,0:T(8,128)(2,1)S(1)}, bf16[112,896]{1,0:T(8,128)(2,1)S(1)}, u32[]{:S(2)}, u32[]{:S(2)}) %collective-permute-start.1) | collective-permute-done | bytes 200736 | tf_op jit(solution)/shard_map/ppermute | solution.py:103
  230.9 0.5 collective-permute-start.3
  231.4 5.4 %collective-permute-start.4 = (bf16[112,896]{1,0:T(8,128)(2,1)S(1)}, bf16[112,896]{1,0:T(8,128)(2,1)S(1)}, u32[]{:S(2)}, u32[]{:S(2)}) collective-permute-start(bf16[112,896]{1,0:T(8,128)(2,1)S(1)} %get-tuple-element.51), channel_id=1, source_target_pairs={{0,2},{1,3},{2,0},{3,1},{4,6},{5,7},{6,4},{7,5},{8,10},{9,11},{10,... | collective-permute-start | bytes 602120 | tf_op jit(solution)/shard_map/ppermute | solution.py:103
  236.9 1.2 collective-permute-done.6
  238.2 3.5 %collective-permute-start.5 = (bf16[112,896]{1,0:T(8,128)(2,1)S(1)}, bf16[112,896]{1,0:T(8,128)(2,1)S(1)}, u32[]{:S(2)}, u32[]{:S(2)}) collective-permute-start(bf16[112,896]{1,0:T(8,128)(2,1)S(1)} %get-tuple-element.50), channel_id=1, source_target_pairs={{0,1},{1,0},{2,3},{3,2},{4,5},{5,4},{6,7},{7,6},{8,9},{9,8},{10,11... | collective-permute-start | bytes 602120 | tf_op jit(solution)/shard_map/ppermute | solution.py:103
  241.7 6.8 %collective-permute-done.7 = bf16[112,896]{1,0:T(8,128)(2,1)S(1)} collective-permute-done((bf16[112,896]{1,0:T(8,128)(2,1)S(1)}, bf16[112,896]{1,0:T(8,128)(2,1)S(1)}, u32[]{:S(2)}, u32[]{:S(2)}) %collective-permute-start.7) | collective-permute-done | bytes 200736 | tf_op jit(solution)/shard_map/ppermute | solution.py:103
  248.6 10.6 %collective-permute-done.3 = bf16[112,896]{1,0:T(8,128)(2,1)S(1)} collective-permute-done((bf16[112,896]{1,0:T(8,128)(2,1)S(1)}, bf16[112,896]{1,0:T(8,128)(2,1)S(1)}, u32[]{:S(2)}, u32[]{:S(2)}) %collective-permute-start.3) | collective-permute-done | bytes 200736 | tf_op jit(solution)/shard_map/ppermute | solution.py:103
  259.2 6.5 %collective-permute-done.4 = bf16[112,896]{1,0:T(8,128)(2,1)S(1)} collective-permute-done((bf16[112,896]{1,0:T(8,128)(2,1)S(1)}, bf16[112,896]{1,0:T(8,128)(2,1)S(1)}, u32[]{:S(2)}, u32[]{:S(2)}) %collective-permute-start.4) | collective-permute-done | bytes 200736 | tf_op jit(solution)/shard_map/ppermute | solution.py:103
  265.8 0.7 add_convert_fusion.2
  266.5 1.7 pad_maximum_fusion.1
  (67 shorter events, 8.2 us)
Async XLA Ops:
  7.5 12.7 %copy-start.14 = (f32[6,256]{1,0:T(8,128)S(1)}, f32[6,256]{1,0:T(8,128)}, u32[]{:S(2)}) copy-start(f32[6,256]{1,0:T(8,128)} %param.6) | copy-start | bytes 18436
  7.5 12.9 %copy-start.15 = (s32[7,3]{0,1:T(4,128)S(1)}, s32[7,3]{0,1:T(4,128)}, u32[]{:S(2)}) copy-start(s32[7,3]{0,1:T(4,128)} %param.7) | copy-start | bytes 256
  7.5 76.8 %all-to-all-start = ((bf16[64,4,2,3,7,112]{5,1,4,2,3,0:T(4,128)(2,1)}), bf16[64,4,2,3,7,112]{5,1,4,2,3,0:T(4,128)(2,1)S(1)}, u32[]{:S(2)}, u32[]{:S(2)}) async-start(bf16[64,4,2,3,7,112]{5,1,4,2,3,0:T(4,128)(2,1)} %copy.48), calls=%async_computation | async-start | bytes 5505024 | tf_op jit(solution)/shard_map/all_to_all | solution.py:62
  20.4 29.4 %copy-start.13 = (s32[256]{0:T(256)}, s32[256]{0:T(256)S(1)}, u32[]{:S(2)}) copy-start(s32[256]{0:T(256)S(1)} %and_select_fusion.3) | copy-start | bytes 3076
  20.4 29.4 %copy-start.11 = (s32[256]{0:T(256)}, s32[256]{0:T(256)S(1)}, u32[]{:S(2)}) copy-start(s32[256]{0:T(256)S(1)} %get-tuple-element.78) | copy-start | bytes 3076
  20.4 29.3 %copy-start.12 = (s32[256]{0:T(256)}, s32[256]{0:T(256)S(1)}, u32[]{:S(2)}) copy-start(s32[256]{0:T(256)S(1)} %get-tuple-element.79) | copy-start | bytes 3076
  87.3 4.6 %copy-start = (bf16[64,4,2,3,7,112]{5,1,0,4,3,2:T(4,128)(2,1)S(1)}, bf16[64,4,2,3,7,112]{5,1,0,4,3,2:T(4,128)(2,1)}, u32[]{:S(2)}) copy-start(bf16[64,4,2,3,7,112]{5,1,0,4,3,2:T(4,128)(2,1)} %copy.49) | copy-start | bytes 7225348
  94.6 1.1 copy-start.3
  94.6 1.4 copy-start.4
  94.6 1.6 copy-start.5
  94.6 1.8 copy-start.6
  94.6 2.1 copy-start.7
  96.7 1.7 copy-start.8
  96.7 1.7 copy-start.9
  96.7 1.7 copy-start.10
  106.6 78.5 %all-to-all-start.1 = ((bf16[256,2,3,7,112]{4,1,3,2,0:T(2,128)(2,1)}), bf16[256,2,3,7,112]{4,1,3,2,0:T(2,128)(2,1)S(1)}, u32[]{:S(2)}, u32[]{:S(2)}) async-start(bf16[256,2,3,7,112]{4,1,3,2,0:T(2,128)(2,1)} %copy.60), calls=%async_computation.1 | async-start | bytes 5505024 | tf_op jit(solution)/shard_map/all_to_all | solution.py:79
  198.5 1.1 copy-start.2
  206.5 14.6 %collective-permute-start = (bf16[112,896]{1,0:T(8,128)(2,1)S(1)}, bf16[112,896]{1,0:T(8,128)(2,1)S(1)}, u32[]{:S(2)}, u32[]{:S(2)}) collective-permute-start(bf16[112,896]{1,0:T(8,128)(2,1)S(1)} %get-tuple-element.49), channel_id=1, source_target_pairs={{0,3},{1,2},{2,1},{3,0},{4,7},{5,6},{6,5},{7,4},{8,11},{9,10},{10,... | collective-permute-start | bytes 602120 | tf_op jit(solution)/shard_map/ppermute | solution.py:103
  207.8 23.0 %collective-permute-start.1 = (bf16[112,896]{1,0:T(8,128)(2,1)S(1)}, bf16[112,896]{1,0:T(8,128)(2,1)S(1)}, u32[]{:S(2)}, u32[]{:S(2)}) collective-permute-start(bf16[112,896]{1,0:T(8,128)(2,1)S(1)} %get-tuple-element.48), channel_id=1, source_target_pairs={{0,2},{1,3},{2,0},{3,1},{4,6},{5,7},{6,4},{7,5},{8,10},{9,11},{10,... | collective-permute-start | bytes 602120 | tf_op jit(solution)/shard_map/ppermute | solution.py:103
  212.9 18.5 %collective-permute-start.2 = (bf16[112,896]{1,0:T(8,128)(2,1)S(1)}, bf16[112,896]{1,0:T(8,128)(2,1)S(1)}, u32[]{:S(2)}, u32[]{:S(2)}) collective-permute-start(bf16[112,896]{1,0:T(8,128)(2,1)S(1)} %get-tuple-element.47), channel_id=1, source_target_pairs={{0,1},{1,0},{2,3},{3,2},{4,5},{5,4},{6,7},{7,6},{8,9},{9,8},{10,11... | collective-permute-start | bytes 602120 | tf_op jit(solution)/shard_map/ppermute | solution.py:103
  214.1 24.0 %collective-permute-start.6 = (bf16[112,896]{1,0:T(8,128)(2,1)S(1)}, bf16[112,896]{1,0:T(8,128)(2,1)S(1)}, u32[]{:S(2)}, u32[]{:S(2)}) collective-permute-start(bf16[112,896]{1,0:T(8,128)(2,1)S(1)} %get-tuple-element.55), channel_id=1, source_target_pairs={{0,3},{1,2},{2,1},{3,0},{4,7},{5,6},{6,5},{7,4},{8,11},{9,10},{10,... | collective-permute-start | bytes 602120 | tf_op jit(solution)/shard_map/ppermute | solution.py:103
  215.0 33.5 %collective-permute-start.7 = (bf16[112,896]{1,0:T(8,128)(2,1)S(1)}, bf16[112,896]{1,0:T(8,128)(2,1)S(1)}, u32[]{:S(2)}, u32[]{:S(2)}) collective-permute-start(bf16[112,896]{1,0:T(8,128)(2,1)S(1)} %get-tuple-element.54), channel_id=1, source_target_pairs={{0,2},{1,3},{2,0},{3,1},{4,6},{5,7},{6,4},{7,5},{8,10},{9,11},{10,... | collective-permute-start | bytes 602120 | tf_op jit(solution)/shard_map/ppermute | solution.py:103
  221.0 27.4 %collective-permute-start.8 = (bf16[112,896]{1,0:T(8,128)(2,1)S(1)}, bf16[112,896]{1,0:T(8,128)(2,1)S(1)}, u32[]{:S(2)}, u32[]{:S(2)}) collective-permute-start(bf16[112,896]{1,0:T(8,128)(2,1)S(1)} %get-tuple-element.53), channel_id=1, source_target_pairs={{0,1},{1,0},{2,3},{3,2},{4,5},{5,4},{6,7},{7,6},{8,9},{9,8},{10,11... | collective-permute-start | bytes 602120 | tf_op jit(solution)/shard_map/ppermute | solution.py:103
  230.9 28.3 %collective-permute-start.3 = (bf16[112,896]{1,0:T(8,128)(2,1)S(1)}, bf16[112,896]{1,0:T(8,128)(2,1)S(1)}, u32[]{:S(2)}, u32[]{:S(2)}) collective-permute-start(bf16[112,896]{1,0:T(8,128)(2,1)S(1)} %get-tuple-element.52), channel_id=1, source_target_pairs={{0,3},{1,2},{2,1},{3,0},{4,7},{5,6},{6,5},{7,4},{8,11},{9,10},{10,... | collective-permute-start | bytes 602120 | tf_op jit(solution)/shard_map/ppermute | solution.py:103
  231.4 34.4 %copy-start.1 = (bf16[3,4,112,896]{3,2,1,0:T(8,128)(2,1)S(1)}, bf16[3,4,112,896]{3,2,1,0:T(8,128)(2,1)}, u32[]{:S(2)}) copy-start(bf16[3,4,112,896]{3,2,1,0:T(8,128)(2,1)} %param.4) | copy-start | bytes 7225348
  231.4 34.3 %collective-permute-start.4 = (bf16[112,896]{1,0:T(8,128)(2,1)S(1)}, bf16[112,896]{1,0:T(8,128)(2,1)S(1)}, u32[]{:S(2)}, u32[]{:S(2)}) collective-permute-start(bf16[112,896]{1,0:T(8,128)(2,1)S(1)} %get-tuple-element.51), channel_id=1, source_target_pairs={{0,2},{1,3},{2,0},{3,1},{4,6},{5,7},{6,4},{7,5},{8,10},{9,11},{10,... | collective-permute-start | bytes 602120 | tf_op jit(solution)/shard_map/ppermute | solution.py:103
  238.2 27.5 %collective-permute-start.5 = (bf16[112,896]{1,0:T(8,128)(2,1)S(1)}, bf16[112,896]{1,0:T(8,128)(2,1)S(1)}, u32[]{:S(2)}, u32[]{:S(2)}) collective-permute-start(bf16[112,896]{1,0:T(8,128)(2,1)S(1)} %get-tuple-element.50), channel_id=1, source_target_pairs={{0,1},{1,0},{2,3},{3,2},{4,5},{5,4},{6,7},{7,6},{8,9},{9,8},{10,11... | collective-permute-start | bytes 602120 | tf_op jit(solution)/shard_map/ppermute | solution.py:103

commit v3 on v2

v3 whole, which is shorter than its diff:
```python
import math

import jax
import jax.numpy as jnp
from jax import lax
from jax.experimental import pallas as pl
from jax.experimental.pallas import tpu as pltpu
from jax.sharding import PartitionSpec as P

NB = 7
MX = 8
LANES = 128


step_length = 0.25


def mesh_coords(momenta, mesh_y, mesh_z):
    flat_index = jnp.arange(momenta, dtype=jnp.int32)
    coord_x = flat_index // (mesh_y * mesh_z)
    coord_y = flat_index // mesh_z % mesh_y
    coord_z = flat_index % mesh_z
    return (coord_x, coord_y, coord_z)


def phase_tables(momenta, mesh_x, mesh_y, mesh_z):
    coord_x, coord_y, coord_z = mesh_coords(momenta, mesh_y, mesh_z)
    phase_index = (
        coord_x[:, None] * coord_x[None, :] * (mesh_y * mesh_z)
        + coord_y[:, None] * coord_y[None, :] * (mesh_x * mesh_z)
        + coord_z[:, None] * coord_z[None, :] * (mesh_x * mesh_y)
    ) % momenta
    angles = phase_index.astype(jnp.float32) * (2.0 * math.pi / momenta)
    cosine = jnp.cos(angles)
    sine_part = jnp.sin(angles)
    forward = jnp.stack([jnp.stack([cosine, sine_part], 1), jnp.stack([-sine_part, cosine], 1)]) * (
        1.0 / momenta
    )
    backward = jnp.stack([jnp.stack([cosine, -sine_part], 1), jnp.stack([sine_part, cosine], 1)])
    return (forward.astype(jnp.bfloat16), backward.astype(jnp.bfloat16))


def pieces_of(values, axis):
    high = lax.reduce_precision(values, 8, 7)
    rest = values - high
    middle = lax.reduce_precision(rest, 8, 7)
    return jnp.concatenate([high, middle, rest - middle], axis=axis).astype(jnp.bfloat16)


def shifted_slots(bond_offsets, sign, sides):
    mesh_x, mesh_y, mesh_z = sides
    coords = mesh_coords(mesh_x * mesh_y * mesh_z, mesh_y, mesh_z)
    slot = 0
    for axis, side in enumerate(sides):
        moved = jnp.mod(coords[axis][None, :] + sign * bond_offsets[:, axis][:, None], side)
        slot = slot * side + moved
    return slot


def shifted_weights(mixing, bond_offsets, column_bonds, row_count, sides):
    count, momenta = mixing.shape
    f32 = jnp.float32
    slots = shifted_slots(bond_offsets, 1, sides)
    source = lax.broadcasted_iota(jnp.int32, (momenta, NB, momenta), 0)
    picks = (source == slots[None]).astype(jnp.bfloat16).reshape(momenta, NB * momenta)
    first = jnp.dot(pieces_of(mixing, 0), picks, preferred_element_type=f32)
    first = first[:count] + first[count : 2 * count] + first[2 * count :]
    first = first.reshape(count * NB, momenta)
    row = lax.broadcasted_iota(jnp.int32, (count * NB, count * LANES), 0)
    lane = lax.broadcasted_iota(jnp.int32, (count * NB, count * LANES), 1)
    spot = lane % LANES
    spread = (row == lane // LANES * NB + spot % NB) & (spot < row_count)
    spread = spread.astype(jnp.bfloat16)
    wide = jnp.dot(pieces_of(first.T, 0), spread, preferred_element_type=f32)
    wide = wide[:momenta] + wide[momenta : 2 * momenta] + wide[2 * momenta :]
    slots = shifted_slots(column_bonds, -1, sides).reshape(NB * momenta)
    target = lax.broadcasted_iota(jnp.int32, (NB * momenta, momenta), 1)
    picks = (target == slots[:, None]).astype(jnp.bfloat16)
    both = jnp.dot(picks, pieces_of(wide, 1), preferred_element_type=f32)
    width = count * LANES
    both = both[:, :width] + both[:, width : 2 * width] + both[:, 2 * width :]
    return both.reshape(NB, momenta, width)


def spread_kernel(v_ref, out_ref, tmp_ref):
    _, mesh_z, row_count, width = v_ref.shape
    groups = out_ref.shape[0]
    narrow = out_ref.shape[1]
    order = width // 2
    for z in range(mesh_z):
        block = v_ref[0, z].astype(jnp.float32)
        block = jnp.concatenate([block, jnp.zeros((LANES - row_count, width), jnp.float32)], axis=0)
        turned = block.T
        for p in range(2):
            for n in range(narrow):
                start = p * order + n * groups
                tmp_ref[n, pl.ds(2 * z + p, groups, stride=2 * mesh_z), :] = turned[
                    start : start + groups
                ]
    for n in range(narrow):
        out_ref[:, n] = tmp_ref[n].reshape(groups, 2 * mesh_z, LANES).astype(jnp.bfloat16)


def spread_rows(vertex, groups):
    _, mesh_z, row_count, width = vertex.shape
    narrow = width // 2 // groups
    return pl.pallas_call(
        spread_kernel,
        grid=(3,),
        in_specs=[pl.BlockSpec((1, mesh_z, row_count, width), lambda t: (t, 0, 0, 0))],
        out_specs=pl.BlockSpec((groups, narrow, 2 * mesh_z, LANES), lambda t: (0, t, 0, 0)),
        out_shape=jax.ShapeDtypeStruct((groups, 3 * narrow, 2 * mesh_z, LANES), jnp.bfloat16),
        scratch_shapes=[pltpu.VMEM((narrow, groups * 2 * mesh_z, LANES), jnp.float32)],
        compiler_params=pltpu.CompilerParams(vmem_limit_bytes=32 * 1024 * 1024),
    )(vertex)


def transform_kernel(x_ref, forward_ref, backward_ref, w_ref, out_ref):
    f32, bf16 = jnp.float32, jnp.bfloat16
    rows = forward_ref.shape[0]
    momenta = rows // 2
    x = [x_ref[:, t, 0].astype(f32).reshape(rows, LANES) for t in range(3)]
    x_all = jnp.concatenate([part.astype(bf16) for part in x], axis=1)
    lattice = jnp.dot(forward_ref[...], x_all, preferred_element_type=f32).astype(bf16).astype(f32)
    mixed = []
    for t in range(3):
        first = lattice[:, (t + 1) % 3 * LANES : ((t + 1) % 3 + 1) * LANES]
        second = lattice[:, (t + 2) % 3 * LANES : ((t + 2) % 3 + 1) * LANES]
        w1 = w_ref[0, :, 2 * t * LANES : (2 * t + 1) * LANES]
        w2 = w_ref[0, :, (2 * t + 1) * LANES : (2 * t + 2) * LANES]
        halves = [
            w1 * first[s * momenta : (s + 1) * momenta] + w2 * second[s * momenta : (s + 1) * momenta]
            for s in range(2)
        ]
        mixed.append(jnp.concatenate(halves, axis=0).astype(bf16))
    mixed = jnp.concatenate(mixed, axis=1)
    projected = jnp.dot(backward_ref[...], mixed, preferred_element_type=f32).astype(bf16)
    for t in range(3):
        part = projected[:, t * LANES : (t + 1) * LANES].astype(f32)
        out_ref[t, 0] = (x[t] + part).astype(bf16)


def transform(x, forward, backward, w):
    groups, _, narrow, inner, _ = x.shape
    rows = groups * inner
    width = w.shape[2]
    return pl.pallas_call(
        transform_kernel,
        grid=(narrow,),
        in_specs=[
            pl.BlockSpec((groups, 3, 1, inner, LANES), lambda n: (0, 0, n, 0, 0)),
            pl.BlockSpec((rows, rows), lambda n: (0, 0)),
            pl.BlockSpec((rows, rows), lambda n: (0, 0)),
            pl.BlockSpec((1, rows // 2, width), lambda n: (n, 0, 0)),
        ],
        out_specs=pl.BlockSpec((3, 1, rows, LANES), lambda n: (0, n, 0, 0)),
        out_shape=jax.ShapeDtypeStruct((3, narrow, rows, LANES), jnp.bfloat16),
        compiler_params=pltpu.CompilerParams(vmem_limit_bytes=32 * 1024 * 1024),
    )(x, forward, backward, w)


def products_kernel(u_ref, loop_ref, out_ref, tall_ref, wide_ref):
    f32, bf16 = jnp.float32, jnp.bfloat16
    narrow, _, cols, groups, _ = u_ref.shape
    order = narrow * groups
    depth = cols * LANES
    row_count = out_ref.shape[1]
    for n in range(narrow):
        for k in range(cols):
            rows, lanes = n * groups, k * LANES
            real, imag = u_ref[n, 0, k], u_ref[n, 1, k]
            tall_ref[rows : rows + groups, lanes : lanes + LANES] = real
            tall_ref[order + rows : order + rows + groups, lanes : lanes + LANES] = imag
            wide_ref[rows : rows + groups, lanes : lanes + LANES] = real
            wide_ref[rows : rows + groups, depth + lanes : depth + lanes + LANES] = -imag
            wide_ref[order + rows : order + rows + groups, lanes : lanes + LANES] = imag
            wide_ref[order + rows : order + rows + groups, depth + lanes : depth + lanes + LANES] = real
    middle = lax.dot_general(
        tall_ref[...], loop_ref[0], (((0,), (0,)), ((), ())), preferred_element_type=f32
    ).astype(bf16)
    change = lax.dot_general(
        middle, wide_ref[...], (((1,), (1,)), ((), ())), preferred_element_type=f32
    )
    increment = (step_length * change).astype(bf16)
    for k in range(cols):
        out_ref[k] = increment[k * LANES : k * LANES + row_count]


def products(t, u, loops, row_count):
    _, _, cols, groups, _ = u.shape
    narrow = u.shape[0] // 3
    rows, depth = loops.shape[1:]
    return pl.pallas_call(
        products_kernel,
        grid=(1,),
        in_specs=[
            pl.BlockSpec((narrow, 2, cols, groups, LANES), lambda i: (t, 0, 0, 0, 0)),
            pl.BlockSpec((1, rows, depth), lambda i: (t, 0, 0)),
        ],
        out_specs=pl.BlockSpec((cols, row_count, rows), lambda i: (0, 0, 0)),
        out_shape=jax.ShapeDtypeStruct((cols, row_count, rows), jnp.bfloat16),
        scratch_shapes=[
            pltpu.VMEM((rows, depth // 2), jnp.bfloat16),
            pltpu.VMEM((rows, depth), jnp.bfloat16),
        ],
        compiler_params=pltpu.CompilerParams(vmem_limit_bytes=32 * 1024 * 1024),
    )(u, loops)


def per_device(vertex, loop_blocks, mixing, bond_offsets):
    groups = lax.axis_size("pb")
    cols = lax.axis_size("col")
    mesh_z = vertex.shape[1]
    row_count = vertex.shape[2]
    order = vertex.shape[3] // 2
    narrow = order // groups
    momenta = mesh_z * groups
    mesh_y = groups // MX
    sent = spread_rows(vertex, groups)
    gathered = lax.all_to_all(sent, "pb", split_axis=0, concat_axis=0, tiled=True)

    forward, backward = phase_tables(momenta, MX, mesh_y, mesh_z)
    forward = forward.transpose(2, 3, 1, 0).reshape(2 * momenta, 2 * momenta)
    backward = backward.transpose(3, 2, 0, 1).reshape(2 * momenta, 2 * momenta)
    bond = jnp.arange(NB, dtype=jnp.int32)
    own = (jnp.arange(narrow, dtype=jnp.int32) * groups + lax.axis_index("pb")) % NB
    column_bonds = jnp.sum(
        jnp.where((own[:, None] == bond[None, :])[:, :, None], bond_offsets[None], 0), axis=1
    )
    w = shifted_weights(mixing, bond_offsets, column_bonds, row_count, (MX, mesh_y, mesh_z))
    lane_pad = LANES - row_count
    loops = loop_blocks.reshape(3, order, 2, cols, row_count)
    loops = jnp.pad(loops, [(0, 0)] * 4 + [(0, lane_pad)]).reshape(3, order, 2, cols * LANES)
    loop_re, loop_im = loops[:, :, 0], loops[:, :, 1]
    loops = jnp.concatenate(
        [
            jnp.concatenate([loop_re, loop_im], axis=2),
            jnp.concatenate([-loop_im, loop_re], axis=2),
        ],
        axis=1,
    )

    gathered = gathered.reshape(groups, 3, narrow, 2 * mesh_z, LANES)
    united = transform(gathered, forward, backward, w)
    united = united.reshape(3 * narrow, momenta, 2, LANES).transpose(1, 0, 2, 3)
    sent = lax.all_to_all(united, ("pb", "col"), split_axis=0, concat_axis=0, tiled=True)
    u = sent.reshape(groups, cols, 3 * narrow, 2, LANES).transpose(2, 3, 1, 0, 4)
    mine = lax.axis_index("col")
    outs = []
    for t in range(3):
        increment = products(t, u, loops, row_count)
        pieces = []
        for k in range(cols):
            piece = lax.dynamic_index_in_dim(increment, mine ^ k, 0, keepdims=False)
            if k:
                piece = lax.ppermute(piece, "col", [(i, i ^ k) for i in range(cols)])
            pieces.append(piece)
        low, high = (mine & 1) == 1, (mine & 2) == 2
        a, b, c, d = pieces
        a, b = jnp.where(low, b, a), jnp.where(low, a, b)
        c, d = jnp.where(low, d, c), jnp.where(low, c, d)
        a, c = jnp.where(high, c, a), jnp.where(high, a, c)
        b, d = jnp.where(high, d, b), jnp.where(high, b, d)
        returned = jnp.stack([a, b, c, d])
        outs.append(
            (vertex[t].astype(jnp.float32) + returned.astype(jnp.float32)).astype(jnp.bfloat16)
        )
    return jnp.stack(outs)


def solution(mesh):
    return jax.shard_map(
        per_device,
        mesh=mesh,
        in_specs=(P(None, "pb", "col", None), P(None, ("pb", "col"), None, None), P(), P()),
        out_specs=P(None, "pb", "col", None),
        check_vma=False,
    )
```

time: 269 us -> 247 us (0.918)
  local copies, waits for them, and re-layouts: 86.9 us -> 37 us
  Pallas kernels: 0 us -> 15.9 us
  waiting for transfers between devices: 109 us -> 121 us
  other arithmetic: 11.5 us -> 19.2 us
  matrix products: 15.7 us -> 8.14 us
    gather x2 -> x0, local copies, waits for them, and re-layouts: 28.8 us -> none  [shifted_weights(): return jnp.take(mixing, flat_slot, axis=1)]
    all_to_all x1, waiting for transfers between devices: 7.42 us -> 35.5 us  [per_device(): lax.all_to_all(sent, 'pb', split_axis=0, concat_axis=0, tiled=True)]
    another operation x12 -> x0, local copies, waits for them, and re-layouts: 22.3 us -> none  [per_device(): w = jnp.tile(weights.transpose(0, 3, 2, 1), (1, 1, 1, row_count // NB))]
    all_to_all x1, waiting for transfers between devices: 66.3 us -> 48.6 us  [per_device(): lax.all_to_all(united, ('pb', 'col'), split_axis=0, concat_axis=0, tiled=...]
    pallas_call x0 -> x5, Pallas kernels: none -> 15.9 us  [the longest x3 7.7 us: products(): pl.pallas_call(products_kernel, grid=(1,), in_specs=[pl.BlockSpec((narrow...]
    reshape x2 -> x7, local copies, waits for them, and re-layouts: 9.19 us -> 22 us  [the longest x2 8.65 us: per_device(): loops = loop_blocks.reshape(3, order, 2, cols, row_count)]
    add x0 -> x5, other arithmetic: none -> 9.3 us  [the longest x1 9.24 us: shifted_weights(): both = both[:, :width] + both[:, width:2 * width] + both[:, 2 * width:]]
    dot_general x20 -> x3, matrix products: 15.7 us -> 8.14 us  [the longest x1 7.2 us: shifted_weights(): both = jnp.dot(picks, pieces_of(wide, 1), preferred_element_type=f32)]
  transfers between devices with their start and end apart: 11 -> 11, of which waited for: 8 -> 8; matrix products, arithmetic and copies ran while one was open for 23% -> 19% of each run, Pallas kernels for 0% -> 0%
where the time goes in v3:
time: 247 us
  waiting for transfers between devices  121 us (49%)
  starting transfers between devices  45.7 us (19%)
  local copies, waits for them, and re-layouts  37 us (15%)
  other arithmetic  19.2 us (8%)
  Pallas kernels  15.9 us (6%)
  matrix products  8.14 us (3%)
    all_to_all x1, waiting for transfers between devices, per_device(): lax.all_to_all(united, ('pb', 'col'), split_axis=0, concat_axis=0, tiled=...  48.6 us
    ppermute x9, waiting for transfers between devices, per_device(): piece = lax.ppermute(piece, 'col', [(i, i ^ k) for i in range(cols)])  36.4 us
    all_to_all x1, waiting for transfers between devices, per_device(): lax.all_to_all(sent, 'pb', split_axis=0, concat_axis=0, tiled=True)  35.5 us
    ppermute x9, starting transfers between devices, per_device(): piece = lax.ppermute(piece, 'col', [(i, i ^ k) for i in range(cols)])  22.4 us
    all_to_all x1, starting transfers between devices, per_device(): lax.all_to_all(sent, 'pb', split_axis=0, concat_axis=0, tiled=True)  12.7 us
    all_to_all x1, starting transfers between devices, per_device(): lax.all_to_all(united, ('pb', 'col'), split_axis=0, concat_axis=0, tiled=...  10.6 us
    unnamed x20, local copies, waits for them, and re-layouts  9.57 us
    add x1, other arithmetic, shifted_weights(): both = both[:, :width] + both[:, width:2 * width] + both[:, 2 * width:]  9.24 us
  transfers between devices with their start and end apart: 11, of which 8 were waited for; matrix products, arithmetic and copies ran while one was open for 19% of the time, Pallas kernels for 0%

profile of v3, /device:TPU:1, one launch (start us, length us, event | category | flops | bytes accessed | tf_op | source)
XLA Modules:
  0.0 246.8 jit_solution(9425669528018250733)
XLA Ops:
  0.0 1.7 copy-done.3
  1.7 1.9 shard_map.46
  3.6 1.5 copy-done.2
  5.1 12.7 %all-to-all-start = ((bf16[64,21,8,128]{3,2,1,0:T(8,128)(2,1)}), bf16[64,21,8,128]{3,2,1,0:T(8,128)(2,1)S(1)}, u32[]{:S(2)}, u32[]{:S(2)}) async-start(bf16[64,21,8,128]{3,2,1,0:T(8,128)(2,1)} %copy-done.2), calls=%async_computation | async-start | bytes 5505024 | tf_op jit(solution)/shard_map/all_to_all | solution.py:220
  17.9 0.1 iota_compare_fusion.4
  17.9 0.1 broadcast_reduce_fusion
  18.1 0.1 select_reduce_fusion
  18.2 0.1 add.498
  18.3 0.1 add.505
  18.5 0.1 broadcast_reduce_fusion.2
  18.7 0.4 fusion.1
  19.1 0.6 reshape.912
  19.7 2.1 fusion.42
  21.9 1.2 copy.25
  23.1 1.1 copy.34
  24.2 1.2 maximum_bitcast_fusion
  25.4 0.1 fusion.11
  25.5 0.5 copy.24
  26.1 0.9 copy.33
  27.0 2.1 copy.26.forward_ref
  29.1 0.5 fusion.20
  29.6 0.2 reduce-precision_convert_fusion.1
  29.8 0.2 reduce-precision_convert_fusion
  30.0 7.2 %fusion = f32[1792,2304]{1,0:T(8,128)} fusion(bf16[256,768]{0,1:T(8,128)(2,1)S(1)} %get-tuple-element.34, bf16[256,768]{0,1:T(8,128)(2,1)S(1)} %get-tuple-element.33, bf16[256,768]{0,1:T(8,128)(2,1)S(1)} %get-tuple-element.5, s32[1792]{0:T(1024)S(1)} %get-tuple-element.42), kind=kOutput, calls=%fused_computation.8 | convolution fusion | flops 2117926912 | bytes 17701888 | tf_op jit(solution)/shard_map/dot_general | solution.py:79
  37.2 9.2 %slice_add_fusion = f32[1792,768]{1,0:T(8,128)} fusion(f32[1792,2304]{1,0:T(8,128)} %fusion), kind=kLoop, calls=%fused_computation | loop fusion | flops 2752512 | bytes 22020096 | tf_op jit(solution)/shard_map/add | solution.py:81
  46.4 35.5 %all-to-all-done = bf16[64,21,8,128]{3,2,1,0:T(8,128)(2,1)S(1)} async-done(((bf16[64,21,8,128]{3,2,1,0:T(8,128)(2,1)}), bf16[64,21,8,128]{3,2,1,0:T(8,128)(2,1)S(1)}, u32[]{:S(2)}, u32[]{:S(2)}) %all-to-all-start) | async-done | bytes 2752544 | tf_op jit(solution)/shard_map/all_to_all | solution.py:220
  81.9 2.6 %copy-done.1 = f32[1792,768]{1,0:T(8,128)S(1)} copy-done((f32[1792,768]{1,0:T(8,128)S(1)}, f32[1792,768]{1,0:T(8,128)}, u32[]{:S(2)}) %copy-start.1) | copy-done | bytes 5505048
  84.5 1.0 copy-done.5
  85.5 6.3 %shard_map.47 = bf16[3,7,512,128]{3,2,1,0:T(8,128)(2,1)S(1)} custom-call(bf16[64,3,7,8,128]{4,3,2,1,0:T(8,128)(2,1)S(1)} %bitcast.138, bf16[512,512]{1,0:T(8,128)(2,1)S(1)} %copy-done.5, bf16[512,512]{1,0:T(8,128)(2,1)S(1)} %bitcast.140, f32[7,256,768]{2,1,0:T(8,128)S(1)} %bitcast.137), custom_call_target="tpu_custom_call" | custom-call | tf_op jit(solution)/shard_map/pallas_call | solution.py:147
  91.8 3.5 %copy.38 = bf16[21,256,2,128]{3,2,0,1:T(2,128)(2,1)} copy(bf16[21,256,2,128]{3,2,1,0:T(2,128)(2,1)S(1)} %bitcast.139) | data formatting | bytes 5505024 | tf_op jit(solution)/shard_map/reshape | solution.py:245
  95.4 10.6 %all-to-all-start.1 = ((bf16[256,21,2,128]{3,2,1,0:T(2,128)(2,1)}), bf16[256,21,2,128]{3,2,1,0:T(2,128)(2,1)}, u32[]{:S(2)}, u32[]{:S(2)}) async-start(bf16[256,21,2,128]{3,2,1,0:T(2,128)(2,1)} %bitcast.133), calls=%async_computation.1 | async-start | bytes 5505024 | tf_op jit(solution)/shard_map/all_to_all | solution.py:246
  106.0 7.7 %reshape.916 = bf16[3,448,2,4,112]{4,3,2,1,0:T(4,128)(2,1)S(1)} reshape(bf16[3,1,448,896]{3,2,1,0:T(8,128)(2,1)} %param.5) | data formatting | bytes 4816896 | tf_op jit(solution)/shard_map/reshape | solution.py:232
  113.7 0.9 copy.30
  114.7 2.9 %pad.4 = bf16[3,448,2,4,128]{4,3,1,0,2:T(4,128)(2,1)} pad(bf16[3,448,2,4,112]{4,3,1,0,2:T(4,128)(2,1)S(1)} %copy.30, bf16[]{:T(256)} %constant.228.clone.1), padding=0_0x0_0x0_0x0_0x0_16 | pad | bytes 5160962 | tf_op jit(solution)/shard_map/jit(_pad)/pad | solution.py:233
  117.6 4.4 %reshape.917 = bf16[3,448,2,512]{3,1,0,2:T(8,128)(2,1)S(1)} reshape(bf16[3,448,2,4,128]{4,3,1,0,2:T(4,128)(2,1)} %pad.4) | data formatting | bytes 5505024 | tf_op jit(solution)/shard_map/reshape | solution.py:233
  122.1 0.1 fusion.80
  122.2 0.2 slice_bitcast_fusion
  122.3 3.0 %maximum_maximum_fusion.loop_ref = bf16[3,896,1024]{2,1,0:T(8,128)(2,1)} fusion(bf16[3,448,512]{2,1,0:T(8,128)(2,1)S(1)} %get-tuple-element.8, bf16[3,448,512]{2,1,0:T(8,128)(2,1)S(1)} %fusion.80, bf16[3,448,512]{2,1,0:T(8,128)(2,1)S(1)} %get-tuple-element.7), kind=kLoop, calls=%fused_computation.2 | loop fusion | flops 22020096 | bytes 9633792 | tf_op jit(solution)/shard_map/concatenate | solution.py:235
  125.4 48.6 %all-to-all-done.1 = bf16[256,21,2,128]{3,2,1,0:T(2,128)(2,1)} async-done(((bf16[256,21,2,128]{3,2,1,0:T(2,128)(2,1)}), bf16[256,21,2,128]{3,2,1,0:T(2,128)(2,1)}, u32[]{:S(2)}, u32[]{:S(2)}) %all-to-all-start.1) | async-done | bytes 2752544 | tf_op jit(solution)/shard_map/all_to_all | solution.py:246
  173.9 2.6 %copy.37 = bf16[64,4,21,2,128]{4,0,1,3,2:T(8,128)(2,1)S(1)} copy(bf16[64,4,21,2,128]{4,3,2,1,0:T(2,128)(2,1)} %bitcast.17) | data formatting | bytes 5505024 | tf_op jit(solution)/shard_map/reshape | solution.py:247
  176.6 0.7 copy-done
  177.3 2.6 %shard_map.49 = bf16[4,112,896]{2,1,0:T(8,128)(2,1)S(1)} custom-call(bf16[21,2,4,64,128]{4,3,2,1,0:T(8,128)(2,1)S(1)} %bitcast.134, bf16[3,896,1024]{2,1,0:T(8,128)(2,1)S(1)} %copy-done), custom_call_target="tpu_custom_call" | custom-call | tf_op jit(solution)/shard_map/pallas_call | solution.py:193
  179.9 2.6 %shard_map.50 = bf16[4,112,896]{2,1,0:T(8,128)(2,1)S(1)} custom-call(bf16[21,2,4,64,128]{4,3,2,1,0:T(8,128)(2,1)S(1)} %bitcast.135, bf16[3,896,1024]{2,1,0:T(8,128)(2,1)S(1)} %copy-done), custom_call_target="tpu_custom_call" | custom-call | tf_op jit(solution)/shard_map/pallas_call | solution.py:193
  182.5 2.6 %shard_map.48 = bf16[4,112,896]{2,1,0:T(8,128)(2,1)S(1)} custom-call(bf16[21,2,4,64,128]{4,3,2,1,0:T(8,128)(2,1)S(1)} %bitcast.136, bf16[3,896,1024]{2,1,0:T(8,128)(2,1)S(1)} %copy-done), custom_call_target="tpu_custom_call" | custom-call | tf_op jit(solution)/shard_map/pallas_call | solution.py:193
  185.0 0.1 dynamic-slice_bitcast_fusion.3
  185.1 1.4 collective-permute-start.3
  186.5 5.0 %collective-permute-start.4 = (bf16[112,896]{1,0:T(8,128)(2,1)S(1)}, bf16[112,896]{1,0:T(8,128)(2,1)S(1)}, u32[]{:S(2)}, u32[]{:S(2)}) collective-permute-start(bf16[112,896]{1,0:T(8,128)(2,1)S(1)} %get-tuple-element.28), channel_id=1, source_target_pairs={{0,2},{1,3},{2,0},{3,1},{4,6},{5,7},{6,4},{7,5},{8,10},{9,11},{10,... | collective-permute-start | bytes 602120 | tf_op jit(solution)/shard_map/ppermute | solution.py:256
  191.5 0.8 collective-permute-start.6
  192.4 5.0 %collective-permute-start.7 = (bf16[112,896]{1,0:T(8,128)(2,1)S(1)}, bf16[112,896]{1,0:T(8,128)(2,1)S(1)}, u32[]{:S(2)}, u32[]{:S(2)}) collective-permute-start(bf16[112,896]{1,0:T(8,128)(2,1)S(1)} %get-tuple-element.31), channel_id=1, source_target_pairs={{0,2},{1,3},{2,0},{3,1},{4,6},{5,7},{6,4},{7,5},{8,10},{9,11},{10,... | collective-permute-start | bytes 602120 | tf_op jit(solution)/shard_map/ppermute | solution.py:256
  197.4 2.2 collective-permute-done.3
  199.7 0.7 collective-permute-start.8
  200.3 9.2 %collective-permute-done.4 = bf16[112,896]{1,0:T(8,128)(2,1)S(1)} collective-permute-done((bf16[112,896]{1,0:T(8,128)(2,1)S(1)}, bf16[112,896]{1,0:T(8,128)(2,1)S(1)}, u32[]{:S(2)}, u32[]{:S(2)}) %collective-permute-start.4) | collective-permute-done | bytes 200736 | tf_op jit(solution)/shard_map/ppermute | solution.py:256
  209.5 0.5 collective-permute-start
  210.0 5.4 %collective-permute-start.1 = (bf16[112,896]{1,0:T(8,128)(2,1)S(1)}, bf16[112,896]{1,0:T(8,128)(2,1)S(1)}, u32[]{:S(2)}, u32[]{:S(2)}) collective-permute-start(bf16[112,896]{1,0:T(8,128)(2,1)S(1)} %get-tuple-element.25), channel_id=1, source_target_pairs={{0,2},{1,3},{2,0},{3,1},{4,6},{5,7},{6,4},{7,5},{8,10},{9,11},{10,... | collective-permute-start | bytes 602120 | tf_op jit(solution)/shard_map/ppermute | solution.py:256
  215.5 0.1 select_bitcast_fusion.7
  215.6 1.3 collective-permute-done.6
  216.8 3.6 %collective-permute-start.2 = (bf16[112,896]{1,0:T(8,128)(2,1)S(1)}, bf16[112,896]{1,0:T(8,128)(2,1)S(1)}, u32[]{:S(2)}, u32[]{:S(2)}) collective-permute-start(bf16[112,896]{1,0:T(8,128)(2,1)S(1)} %get-tuple-element.24), channel_id=1, source_target_pairs={{0,1},{1,0},{2,3},{3,2},{4,5},{5,4},{6,7},{7,6},{8,9},{9,8},{10,11... | collective-permute-start | bytes 602120 | tf_op jit(solution)/shard_map/ppermute | solution.py:256
  220.4 6.7 %collective-permute-done.7 = bf16[112,896]{1,0:T(8,128)(2,1)S(1)} collective-permute-done((bf16[112,896]{1,0:T(8,128)(2,1)S(1)}, bf16[112,896]{1,0:T(8,128)(2,1)S(1)}, u32[]{:S(2)}, u32[]{:S(2)}) %collective-permute-start.7) | collective-permute-done | bytes 200736 | tf_op jit(solution)/shard_map/ppermute | solution.py:256
  227.2 0.1 select_bitcast_fusion.3
  227.3 10.6 %collective-permute-done = bf16[112,896]{1,0:T(8,128)(2,1)S(1)} collective-permute-done((bf16[112,896]{1,0:T(8,128)(2,1)S(1)}, bf16[112,896]{1,0:T(8,128)(2,1)S(1)}, u32[]{:S(2)}, u32[]{:S(2)}) %collective-permute-start) | collective-permute-done | bytes 200736 | tf_op jit(solution)/shard_map/ppermute | solution.py:256
  237.9 6.4 %collective-permute-done.1 = bf16[112,896]{1,0:T(8,128)(2,1)S(1)} collective-permute-done((bf16[112,896]{1,0:T(8,128)(2,1)S(1)}, bf16[112,896]{1,0:T(8,128)(2,1)S(1)}, u32[]{:S(2)}, u32[]{:S(2)}) %collective-permute-start.1) | collective-permute-done | bytes 200736 | tf_op jit(solution)/shard_map/ppermute | solution.py:256
  244.3 0.1 select_bitcast_fusion.11
  244.4 0.7 add_convert_fusion.2
  245.1 1.7 pad_maximum_fusion
  (46 shorter events, 0.5 us)
Async XLA Ops:
  0.0 1.7 copy-start.3
  3.6 1.5 copy-start.2
  5.1 12.7 %copy-start.8 = (s32[7,3]{0,1:T(4,128)S(1)}, s32[7,3]{0,1:T(4,128)}, u32[]{:S(2)}) copy-start(s32[7,3]{0,1:T(4,128)} %param.7) | copy-start | bytes 256
  5.1 13.5 %copy-start.7 = (f32[6,256]{1,0:T(8,128)S(1)}, f32[6,256]{1,0:T(8,128)}, u32[]{:S(2)}) copy-start(f32[6,256]{1,0:T(8,128)} %param.6) | copy-start | bytes 18436
  5.1 76.8 %all-to-all-start = ((bf16[64,21,8,128]{3,2,1,0:T(8,128)(2,1)}), bf16[64,21,8,128]{3,2,1,0:T(8,128)(2,1)S(1)}, u32[]{:S(2)}, u32[]{:S(2)}) async-start(bf16[64,21,8,128]{3,2,1,0:T(8,128)(2,1)} %copy-done.2), calls=%async_computation | async-start | bytes 5505024 | tf_op jit(solution)/shard_map/all_to_all | solution.py:220
  25.4 3.6 %copy-start.6 = (f32[42,256]{1,0:T(8,128)S(1)}, f32[42,256]{1,0:T(8,128)}, u32[]{:S(2)}) copy-start(f32[42,256]{1,0:T(8,128)} %reshape.912) | copy-start | bytes 129028
  81.9 2.6 %copy-start.1 = (f32[1792,768]{1,0:T(8,128)S(1)}, f32[1792,768]{1,0:T(8,128)}, u32[]{:S(2)}) copy-start(f32[1792,768]{1,0:T(8,128)} %slice_add_fusion) | copy-start | bytes 16515076
  84.5 1.0 copy-start.5
  95.4 78.6 %all-to-all-start.1 = ((bf16[256,21,2,128]{3,2,1,0:T(2,128)(2,1)}), bf16[256,21,2,128]{3,2,1,0:T(2,128)(2,1)}, u32[]{:S(2)}, u32[]{:S(2)}) async-start(bf16[256,21,2,128]{3,2,1,0:T(2,128)(2,1)} %bitcast.133), calls=%async_computation.1 | async-start | bytes 5505024 | tf_op jit(solution)/shard_map/all_to_all | solution.py:246
  173.9 3.4 %copy-start = (bf16[3,896,1024]{2,1,0:T(8,128)(2,1)S(1)}, bf16[3,896,1024]{2,1,0:T(8,128)(2,1)}, u32[]{:S(2)}) copy-start(bf16[3,896,1024]{2,1,0:T(8,128)(2,1)} %maximum_maximum_fusion.loop_ref) | copy-start | bytes 16515076
  185.1 14.6 %collective-permute-start.3 = (bf16[112,896]{1,0:T(8,128)(2,1)S(1)}, bf16[112,896]{1,0:T(8,128)(2,1)S(1)}, u32[]{:S(2)}, u32[]{:S(2)}) collective-permute-start(bf16[112,896]{1,0:T(8,128)(2,1)S(1)} %get-tuple-element.29), channel_id=1, source_target_pairs={{0,3},{1,2},{2,1},{3,0},{4,7},{5,6},{6,5},{7,4},{8,11},{9,10},{10,... | collective-permute-start | bytes 602120 | tf_op jit(solution)/shard_map/ppermute | solution.py:256
  186.5 23.1 %collective-permute-start.4 = (bf16[112,896]{1,0:T(8,128)(2,1)S(1)}, bf16[112,896]{1,0:T(8,128)(2,1)S(1)}, u32[]{:S(2)}, u32[]{:S(2)}) collective-permute-start(bf16[112,896]{1,0:T(8,128)(2,1)S(1)} %get-tuple-element.28), channel_id=1, source_target_pairs={{0,2},{1,3},{2,0},{3,1},{4,6},{5,7},{6,4},{7,5},{8,10},{9,11},{10,... | collective-permute-start | bytes 602120 | tf_op jit(solution)/shard_map/ppermute | solution.py:256
  191.5 18.6 %collective-permute-start.5 = (bf16[112,896]{1,0:T(8,128)(2,1)S(1)}, bf16[112,896]{1,0:T(8,128)(2,1)S(1)}, u32[]{:S(2)}, u32[]{:S(2)}) collective-permute-start(bf16[112,896]{1,0:T(8,128)(2,1)S(1)} %get-tuple-element.27), channel_id=1, source_target_pairs={{0,1},{1,0},{2,3},{3,2},{4,5},{5,4},{6,7},{7,6},{8,9},{9,8},{10,11... | collective-permute-start | bytes 602120 | tf_op jit(solution)/shard_map/ppermute | solution.py:256
  191.5 25.3 %collective-permute-start.6 = (bf16[112,896]{1,0:T(8,128)(2,1)S(1)}, bf16[112,896]{1,0:T(8,128)(2,1)S(1)}, u32[]{:S(2)}, u32[]{:S(2)}) collective-permute-start(bf16[112,896]{1,0:T(8,128)(2,1)S(1)} %get-tuple-element.32), channel_id=1, source_target_pairs={{0,3},{1,2},{2,1},{3,0},{4,7},{5,6},{6,5},{7,4},{8,11},{9,10},{10,... | collective-permute-start | bytes 602120 | tf_op jit(solution)/shard_map/ppermute | solution.py:256
  192.4 34.8 %collective-permute-start.7 = (bf16[112,896]{1,0:T(8,128)(2,1)S(1)}, bf16[112,896]{1,0:T(8,128)(2,1)S(1)}, u32[]{:S(2)}, u32[]{:S(2)}) collective-permute-start(bf16[112,896]{1,0:T(8,128)(2,1)S(1)} %get-tuple-element.31), channel_id=1, source_target_pairs={{0,2},{1,3},{2,0},{3,1},{4,6},{5,7},{6,4},{7,5},{8,10},{9,11},{10,... | collective-permute-start | bytes 602120 | tf_op jit(solution)/shard_map/ppermute | solution.py:256
  199.7 27.5 %collective-permute-start.8 = (bf16[112,896]{1,0:T(8,128)(2,1)S(1)}, bf16[112,896]{1,0:T(8,128)(2,1)S(1)}, u32[]{:S(2)}, u32[]{:S(2)}) collective-permute-start(bf16[112,896]{1,0:T(8,128)(2,1)S(1)} %get-tuple-element.30), channel_id=1, source_target_pairs={{0,1},{1,0},{2,3},{3,2},{4,5},{5,4},{6,7},{7,6},{8,9},{9,8},{10,11... | collective-permute-start | bytes 602120 | tf_op jit(solution)/shard_map/ppermute | solution.py:256
  209.5 28.4 %collective-permute-start = (bf16[112,896]{1,0:T(8,128)(2,1)S(1)}, bf16[112,896]{1,0:T(8,128)(2,1)S(1)}, u32[]{:S(2)}, u32[]{:S(2)}) collective-permute-start(bf16[112,896]{1,0:T(8,128)(2,1)S(1)} %get-tuple-element.26), channel_id=1, source_target_pairs={{0,3},{1,2},{2,1},{3,0},{4,7},{5,6},{6,5},{7,4},{8,11},{9,10},{10,... | collective-permute-start | bytes 602120 | tf_op jit(solution)/shard_map/ppermute | solution.py:256
  210.0 34.4 %copy-start.4 = (bf16[3,4,112,896]{3,2,1,0:T(8,128)(2,1)S(1)}, bf16[3,4,112,896]{3,2,1,0:T(8,128)(2,1)}, u32[]{:S(2)}) copy-start(bf16[3,4,112,896]{3,2,1,0:T(8,128)(2,1)} %v_ref.1) | copy-start | bytes 7225348
  210.0 34.2 %collective-permute-start.1 = (bf16[112,896]{1,0:T(8,128)(2,1)S(1)}, bf16[112,896]{1,0:T(8,128)(2,1)S(1)}, u32[]{:S(2)}, u32[]{:S(2)}) collective-permute-start(bf16[112,896]{1,0:T(8,128)(2,1)S(1)} %get-tuple-element.25), channel_id=1, source_target_pairs={{0,2},{1,3},{2,0},{3,1},{4,6},{5,7},{6,4},{7,5},{8,10},{9,11},{10,... | collective-permute-start | bytes 602120 | tf_op jit(solution)/shard_map/ppermute | solution.py:256
  216.8 27.5 %collective-permute-start.2 = (bf16[112,896]{1,0:T(8,128)(2,1)S(1)}, bf16[112,896]{1,0:T(8,128)(2,1)S(1)}, u32[]{:S(2)}, u32[]{:S(2)}) collective-permute-start(bf16[112,896]{1,0:T(8,128)(2,1)S(1)} %get-tuple-element.24), channel_id=1, source_target_pairs={{0,1},{1,0},{2,3},{3,2},{4,5},{5,4},{6,7},{7,6},{8,9},{9,8},{10,11... | collective-permute-start | bytes 602120 | tf_op jit(solution)/shard_map/ppermute | solution.py:256

commit v4 on v3

--- a/solution.py
+++ b/solution.py
@@ -1,3 +1,4 @@
+import functools
 import math
 
 import jax
@@ -112,51 +113,47 @@
         out_shape=jax.ShapeDtypeStruct((groups, 3 * narrow, 2 * mesh_z, LANES), jnp.bfloat16),
         scratch_shapes=[pltpu.VMEM((narrow, groups * 2 * mesh_z, LANES), jnp.float32)],
         compiler_params=pltpu.CompilerParams(vmem_limit_bytes=32 * 1024 * 1024),
-    )(vertex)
-
-
-def transform_kernel(x_ref, forward_ref, backward_ref, w_ref, out_ref):
+    )(in_hbm(vertex))
+
+
+def transform_kernel(t, x_ref, forward_ref, backward_ref, w_ref, out_ref):
     f32, bf16 = jnp.float32, jnp.bfloat16
     rows = forward_ref.shape[0]
     momenta = rows // 2
-    x = [x_ref[:, t, 0].astype(f32).reshape(rows, LANES) for t in range(3)]
-    x_all = jnp.concatenate([part.astype(bf16) for part in x], axis=1)
-    lattice = jnp.dot(forward_ref[...], x_all, preferred_element_type=f32).astype(bf16).astype(f32)
-    mixed = []
-    for t in range(3):
-        first = lattice[:, (t + 1) % 3 * LANES : ((t + 1) % 3 + 1) * LANES]
-        second = lattice[:, (t + 2) % 3 * LANES : ((t + 2) % 3 + 1) * LANES]
-        w1 = w_ref[0, :, 2 * t * LANES : (2 * t + 1) * LANES]
-        w2 = w_ref[0, :, (2 * t + 1) * LANES : (2 * t + 2) * LANES]
-        halves = [
-            w1 * first[s * momenta : (s + 1) * momenta] + w2 * second[s * momenta : (s + 1) * momenta]
-            for s in range(2)
-        ]
-        mixed.append(jnp.concatenate(halves, axis=0).astype(bf16))
-    mixed = jnp.concatenate(mixed, axis=1)
+    x = [x_ref[:, i, 0].astype(f32).reshape(rows, LANES) for i in range(3)]
+    pair = jnp.concatenate([x[(t + 1) % 3].astype(bf16), x[(t + 2) % 3].astype(bf16)], axis=1)
+    lattice = jnp.dot(forward_ref[...], pair, preferred_element_type=f32).astype(bf16).astype(f32)
+    halves = []
+    for s in range(2):
+        half = lattice[s * momenta : (s + 1) * momenta]
+        halves.append(
+            w_ref[0, :, :LANES] * half[:, :LANES] + w_ref[0, :, LANES:] * half[:, LANES:]
+        )
+    mixed = jnp.concatenate(halves, axis=0).astype(bf16)
     projected = jnp.dot(backward_ref[...], mixed, preferred_element_type=f32).astype(bf16)
-    for t in range(3):
-        part = projected[:, t * LANES : (t + 1) * LANES].astype(f32)
-        out_ref[t, 0] = (x[t] + part).astype(bf16)
-
-
-def transform(x, forward, backward, w):
+    out_ref[0] = (x[t] + projected.astype(f32)).astype(bf16)
+
+
+def in_hbm(array):
+    return pltpu.with_memory_space_constraint(array, pltpu.HBM)
+
+
+def transform(t, x, forward, backward, w):
     groups, _, narrow, inner, _ = x.shape
     rows = groups * inner
-    width = w.shape[2]
     return pl.pallas_call(
-        transform_kernel,
+        functools.partial(transform_kernel, t),
         grid=(narrow,),
         in_specs=[
             pl.BlockSpec((groups, 3, 1, inner, LANES), lambda n: (0, 0, n, 0, 0)),
             pl.BlockSpec((rows, rows), lambda n: (0, 0)),
             pl.BlockSpec((rows, rows), lambda n: (0, 0)),
-            pl.BlockSpec((1, rows // 2, width), lambda n: (n, 0, 0)),
-        ],
-        out_specs=pl.BlockSpec((3, 1, rows, LANES), lambda n: (0, n, 0, 0)),
-        out_shape=jax.ShapeDtypeStruct((3, narrow, rows, LANES), jnp.bfloat16),
+            pl.BlockSpec((1, rows // 2, 2 * LANES), lambda n: (n, 0, t)),
+        ],
+        out_specs=pl.BlockSpec((1, rows, LANES), lambda n: (n, 0, 0)),
+        out_shape=jax.ShapeDtypeStruct((narrow, rows, LANES), jnp.bfloat16),
         compiler_params=pltpu.CompilerParams(vmem_limit_bytes=32 * 1024 * 1024),
-    )(x, forward, backward, w)
+    )(x, forward, backward, in_hbm(w))
 
 
 def products_kernel(u_ref, loop_ref, out_ref, tall_ref, wide_ref):
@@ -188,13 +185,13 @@
 
 def products(t, u, loops, row_count):
     _, _, cols, groups, _ = u.shape
-    narrow = u.shape[0] // 3
+    narrow = u.shape[0]
     rows, depth = loops.shape[1:]
     return pl.pallas_call(
         products_kernel,
         grid=(1,),
         in_specs=[
-            pl.BlockSpec((narrow, 2, cols, groups, LANES), lambda i: (t, 0, 0, 0, 0)),
+            pl.BlockSpec((narrow, 2, cols, groups, LANES), lambda i: (0, 0, 0, 0, 0)),
             pl.BlockSpec((1, rows, depth), lambda i: (t, 0, 0)),
         ],
         out_specs=pl.BlockSpec((cols, row_count, rows), lambda i: (0, 0, 0)),
@@ -204,7 +201,7 @@
             pltpu.VMEM((rows, depth), jnp.bfloat16),
         ],
         compiler_params=pltpu.CompilerParams(vmem_limit_bytes=32 * 1024 * 1024),
-    )(u, loops)
+    )(u, in_hbm(loops))
 
 
 def per_device(vertex, loop_blocks, mixing, bond_offsets):
@@ -240,14 +237,15 @@
         axis=1,
     )
 
+    gathered, w, loops = lax.optimization_barrier((gathered, w, loops))
     gathered = gathered.reshape(groups, 3, narrow, 2 * mesh_z, LANES)
-    united = transform(gathered, forward, backward, w)
-    united = united.reshape(3 * narrow, momenta, 2, LANES).transpose(1, 0, 2, 3)
-    sent = lax.all_to_all(united, ("pb", "col"), split_axis=0, concat_axis=0, tiled=True)
-    u = sent.reshape(groups, cols, 3 * narrow, 2, LANES).transpose(2, 3, 1, 0, 4)
     mine = lax.axis_index("col")
     outs = []
     for t in range(3):
+        united = transform(t, gathered, forward, backward, w)
+        united = united.reshape(narrow, momenta, 2, LANES).transpose(1, 0, 2, 3)
+        sent = lax.all_to_all(united, ("pb", "col"), split_axis=0, concat_axis=0, tiled=True)
+        u = sent.reshape(groups, cols, narrow, 2, LANES).transpose(2, 3, 1, 0, 4)
         increment = products(t, u, loops, row_count)
         pieces = []
         for k in range(cols):

time: 247 us -> 264 us (1.069)
  the two profiles are of different devices: /device:TPU:1 before, /device:TPU:33 now
where the time goes in v4:
time: 264 us; the launch traced here: 263 us
  waiting for transfers between devices  76.3 us (29%)
  starting transfers between devices  73.7 us (28%)
  local copies, waits for them, and re-layouts  45.3 us (17%)
  Pallas kernels  37.2 us (14%)
  other arithmetic  21.9 us (8%)
  matrix products  8.09 us (3%)
    all_to_all x3, waiting for transfers between devices, per_device(): lax.all_to_all(united, ('pb', 'col'), split_axis=0, concat_axis=0, tiled=...  40.7 us
    ppermute x9, starting transfers between devices, per_device(): piece = lax.ppermute(piece, 'col', [(i, i ^ k) for i in range(cols)])  34.9 us
    all_to_all x3, starting transfers between devices, per_device(): lax.all_to_all(united, ('pb', 'col'), split_axis=0, concat_axis=0, tiled=...  27.6 us
    ppermute x9, waiting for transfers between devices, per_device(): piece = lax.ppermute(piece, 'col', [(i, i ^ k) for i in range(cols)])  25.9 us
    pallas_call x3, Pallas kernels, transform(): pl.pallas_call(functools.partial(transform_kernel, t), grid=(narrow,), in...  21.5 us
    pallas_call x3, Pallas kernels, products(): pl.pallas_call(products_kernel, grid=(1,), in_specs=[pl.BlockSpec((narrow...  12.2 us
    reshape x2, local copies, waits for them, and re-layouts, per_device(): loops = loop_blocks.reshape(3, order, 2, cols, row_count)  11.2 us
    all_to_all x1, starting transfers between devices, per_device(): lax.all_to_all(sent, 'pb', split_axis=0, concat_axis=0, tiled=True)  11.2 us
  transfers between devices with their start and end apart: 13, of which 8 were waited for; matrix products, arithmetic and copies ran while one was open for 24% of the time, Pallas kernels for 10%

profile of v4, /device:TPU:33, one launch (start us, length us, event | category | flops | bytes accessed | tf_op | source)
XLA Modules:
  0.0 263.0 jit_solution(8611394840213035215)
XLA Ops:
  0.0 3.5 %shard_map.46 = bf16[64,21,8,128]{3,2,1,0:T(8,128)(2,1)S(1)} custom-call(bf16[3,4,112,896]{3,2,1,0:T(8,128)(2,1)} %v_ref.1), custom_call_target="tpu_custom_call" | custom-call | tf_op jit(solution)/shard_map/pallas_call | solution.py:108
  3.6 1.6 copy-done
  5.2 11.2 %all-to-all-start = ((bf16[64,21,8,128]{3,2,1,0:T(8,128)(2,1)}), bf16[64,21,8,128]{3,2,1,0:T(8,128)(2,1)S(1)}, u32[]{:S(2)}, u32[]{:S(2)}) async-start(bf16[64,21,8,128]{3,2,1,0:T(8,128)(2,1)} %copy-done), calls=%async_computation | async-start | bytes 5505024 | tf_op jit(solution)/shard_map/all_to_all | solution.py:217
  16.7 0.1 select_reduce_fusion
  17.3 0.4 fusion.1
  17.7 0.6 reshape.921
  18.3 8.5 %reshape.923 = bf16[3,448,2,4,112]{4,3,2,1,0:T(4,128)(2,1)} reshape(bf16[3,1,448,896]{3,2,1,0:T(8,128)(2,1)} %param.5) | data formatting | bytes 4816896 | tf_op jit(solution)/shard_map/reshape | solution.py:229
  26.8 2.7 %copy.38 = bf16[3,448,2,4,112]{4,3,1,0,2:T(4,128)(2,1)S(1)} copy(bf16[3,448,2,4,112]{4,3,2,1,0:T(4,128)(2,1)} %reshape.923) | data formatting | bytes 4816896 | tf_op jit(solution)/shard_map/reshape | solution.py:229
  29.5 3.0 %pad.4 = bf16[3,448,2,4,128]{4,3,1,0,2:T(4,128)(2,1)} pad(bf16[3,448,2,4,112]{4,3,1,0,2:T(4,128)(2,1)S(1)} %copy.38, bf16[]{:T(256)} %constant.223.clone.1), padding=0_0x0_0x0_0x0_0x0_16 | pad | bytes 5160962 | tf_op jit(solution)/shard_map/jit(_pad)/pad | solution.py:230
  32.5 5.6 %reshape.924 = bf16[3,448,2,512]{3,1,0,2:T(8,128)(2,1)} reshape(bf16[3,448,2,4,128]{4,3,1,0,2:T(4,128)(2,1)} %pad.4) | data formatting | bytes 5505024 | tf_op jit(solution)/shard_map/reshape | solution.py:230
  38.1 2.0 fusion.42
  40.3 0.5 copy.39
  40.8 0.9 copy.59
  41.7 1.3 copy.41.forward_ref
  43.0 0.9 maximum_bitcast_fusion.3
  43.9 0.8 maximum_bitcast_fusion.2
  44.8 2.0 copy.40
  46.8 1.9 copy.60
  48.7 0.5 fusion.20
  49.3 0.2 reduce-precision_convert_fusion.1
  49.4 0.2 reduce-precision_convert_fusion
  49.6 1.4 copy-done.4
  51.1 0.3 slice_bitcast_fusion
  51.5 3.0 %maximum_maximum_fusion.loop_ref = bf16[3,896,1024]{2,1,0:T(8,128)(2,1)} fusion(bf16[3,448,512]{2,1,0:T(8,128)(2,1)S(1)} %get-tuple-element.14, bf16[3,448,512]{2,1,0:T(8,128)(2,1)S(1)} %fusion.80, bf16[3,448,512]{2,1,0:T(8,128)(2,1)S(1)} %get-tuple-element.13), kind=kLoop, calls=%fused_computation.2 | loop fusion | flops 22020096 | bytes 9633792 | tf_op jit(solution)/shard_map/concatenate | solution.py:232
  54.5 7.2 %fusion = f32[1792,2304]{1,0:T(8,128)} fusion(bf16[256,768]{0,1:T(8,128)(2,1)S(1)} %get-tuple-element.40, bf16[256,768]{0,1:T(8,128)(2,1)S(1)} %get-tuple-element.39, bf16[256,768]{0,1:T(8,128)(2,1)S(1)} %get-tuple-element.11, s32[1792]{0:T(1024)S(1)} %get-tuple-element.48), kind=kOutput, calls=%fused_computation.6 | convolution fusion | flops 2117926912 | bytes 17701888 | tf_op jit(solution)/shard_map/dot_general | solution.py:80
  61.6 9.3 %slice_add_fusion = f32[1792,768]{1,0:T(8,128)} fusion(f32[1792,2304]{1,0:T(8,128)} %fusion), kind=kLoop, calls=%fused_computation | loop fusion | flops 2752512 | bytes 22020096 | tf_op jit(solution)/shard_map/add | solution.py:82
  70.9 9.7 %all-to-all-done = bf16[64,21,8,128]{3,2,1,0:T(8,128)(2,1)S(1)} async-done(((bf16[64,21,8,128]{3,2,1,0:T(8,128)(2,1)}), bf16[64,21,8,128]{3,2,1,0:T(8,128)(2,1)S(1)}, u32[]{:S(2)}, u32[]{:S(2)}) %all-to-all-start) | async-done | bytes 2752544 | tf_op jit(solution)/shard_map/all_to_all | solution.py:217
  80.7 1.0 copy-done.1
  81.7 7.3 %shard_map.49 = bf16[7,512,128]{2,1,0:T(8,128)(2,1)S(1)} custom-call(bf16[64,3,7,8,128]{4,3,2,1,0:T(8,128)(2,1)S(1)} %bitcast.150, bf16[512,512]{1,0:T(8,128)(2,1)S(1)} %copy.41.forward_ref, bf16[512,512]{1,0:T(8,128)(2,1)S(1)} %bitcast.153, f32[7,256,768]{2,1,0:T(8,128)} %bitcast.162), custom_call_target="tpu_custom_call" | custom-call | tf_op jit(solution)/shard_map/pallas_call | solution.py:144
  89.0 1.6 copy.71
  90.5 11.0 %all-to-all-start.2 = ((bf16[256,7,2,128]{3,2,1,0:T(2,128)(2,1)}), bf16[256,7,2,128]{3,2,1,0:T(2,128)(2,1)}, u32[]{:S(2)}, u32[]{:S(2)}) async-start(bf16[256,7,2,128]{3,2,1,0:T(2,128)(2,1)} %bitcast.166), calls=%async_computation.2 | async-start | bytes 1835008 | tf_op jit(solution)/shard_map/all_to_all | solution.py:247
  101.6 1.0 copy-done.2
  102.6 7.1 %shard_map.51 = bf16[7,512,128]{2,1,0:T(8,128)(2,1)S(1)} custom-call(bf16[64,3,7,8,128]{4,3,2,1,0:T(8,128)(2,1)S(1)} %bitcast.151, bf16[512,512]{1,0:T(8,128)(2,1)S(1)} %copy.41.forward_ref, bf16[512,512]{1,0:T(8,128)(2,1)S(1)} %bitcast.154, f32[7,256,768]{2,1,0:T(8,128)} %bitcast.163), custom_call_target="tpu_custom_call" | custom-call | tf_op jit(solution)/shard_map/pallas_call | solution.py:144
  109.7 1.6 copy.70
  111.3 18.2 %all-to-all-done.2 = bf16[256,7,2,128]{3,2,1,0:T(2,128)(2,1)} async-done(((bf16[256,7,2,128]{3,2,1,0:T(2,128)(2,1)}), bf16[256,7,2,128]{3,2,1,0:T(2,128)(2,1)}, u32[]{:S(2)}, u32[]{:S(2)}) %all-to-all-start.2) | async-done | bytes 917536 | tf_op jit(solution)/shard_map/all_to_all | solution.py:247
  129.5 8.3 %all-to-all-start.3 = ((bf16[256,7,2,128]{3,2,1,0:T(2,128)(2,1)}), bf16[256,7,2,128]{3,2,1,0:T(2,128)(2,1)}, u32[]{:S(2)}, u32[]{:S(2)}) async-start(bf16[256,7,2,128]{3,2,1,0:T(2,128)(2,1)} %bitcast.165), calls=%async_computation.3 | async-start | bytes 1835008 | tf_op jit(solution)/shard_map/all_to_all | solution.py:247
  137.8 1.0 copy-done.3
  138.8 7.1 %shard_map.47 = bf16[7,512,128]{2,1,0:T(8,128)(2,1)S(1)} custom-call(bf16[64,3,7,8,128]{4,3,2,1,0:T(8,128)(2,1)S(1)} %bitcast.152, bf16[512,512]{1,0:T(8,128)(2,1)S(1)} %copy.41.forward_ref, bf16[512,512]{1,0:T(8,128)(2,1)S(1)} %bitcast.155, f32[7,256,768]{2,1,0:T(8,128)} %bitcast.164), custom_call_target="tpu_custom_call" | custom-call | tf_op jit(solution)/shard_map/pallas_call | solution.py:144
  145.9 1.6 copy.72
  147.5 18.2 %all-to-all-done.3 = bf16[256,7,2,128]{3,2,1,0:T(2,128)(2,1)} async-done(((bf16[256,7,2,128]{3,2,1,0:T(2,128)(2,1)}), bf16[256,7,2,128]{3,2,1,0:T(2,128)(2,1)}, u32[]{:S(2)}, u32[]{:S(2)}) %all-to-all-start.3) | async-done | bytes 917536 | tf_op jit(solution)/shard_map/all_to_all | solution.py:247
  165.7 8.3 %all-to-all-start.1 = ((bf16[256,7,2,128]{3,2,1,0:T(2,128)(2,1)}), bf16[256,7,2,128]{3,2,1,0:T(2,128)(2,1)}, u32[]{:S(2)}, u32[]{:S(2)}) async-start(bf16[256,7,2,128]{3,2,1,0:T(2,128)(2,1)} %bitcast.149), calls=%async_computation.1 | async-start | bytes 1835008 | tf_op jit(solution)/shard_map/all_to_all | solution.py:247
  174.0 1.4 copy.68
  175.5 4.1 %shard_map.50 = bf16[4,112,896]{2,1,0:T(8,128)(2,1)S(1)} custom-call(bf16[7,2,4,64,128]{4,3,2,1,0:T(8,128)(2,1)S(1)} %bitcast.160, bf16[3,896,1024]{2,1,0:T(8,128)(2,1)} %maximum_maximum_fusion.loop_ref), custom_call_target="tpu_custom_call" | custom-call | tf_op jit(solution)/shard_map/pallas_call | solution.py:190
  179.5 0.9 dynamic-slice_bitcast_fusion.3
  180.4 5.5 %collective-permute-start.3 = (bf16[112,896]{1,0:T(8,128)(2,1)}, bf16[112,896]{1,0:T(8,128)(2,1)S(1)}, u32[]{:S(2)}, u32[]{:S(2)}) collective-permute-start(bf16[112,896]{1,0:T(8,128)(2,1)} %get-tuple-element.35), channel_id=1, source_target_pairs={{0,3},{1,2},{2,1},{3,0},{4,7},{5,6},{6,5},{7,4},{8,11},{9,10},{10,... | collective-permute-start | bytes 602120 | tf_op jit(solution)/shard_map/ppermute | solution.py:254
  186.0 0.4 collective-permute-start.5
  186.4 1.4 copy.67
  187.9 4.1 %shard_map.52 = bf16[4,112,896]{2,1,0:T(8,128)(2,1)S(1)} custom-call(bf16[7,2,4,64,128]{4,3,2,1,0:T(8,128)(2,1)S(1)} %bitcast.161, bf16[3,896,1024]{2,1,0:T(8,128)(2,1)} %maximum_maximum_fusion.loop_ref), custom_call_target="tpu_custom_call" | custom-call | tf_op jit(solution)/shard_map/pallas_call | solution.py:190
  191.9 0.8 dynamic-slice_bitcast_fusion
  192.8 5.2 %collective-permute-start.6 = (bf16[112,896]{1,0:T(8,128)(2,1)}, bf16[112,896]{1,0:T(8,128)(2,1)S(1)}, u32[]{:S(2)}, u32[]{:S(2)}) collective-permute-start(bf16[112,896]{1,0:T(8,128)(2,1)} %get-tuple-element.38), channel_id=1, source_target_pairs={{0,3},{1,2},{2,1},{3,0},{4,7},{5,6},{6,5},{7,4},{8,11},{9,10},{10,... | collective-permute-start | bytes 602120 | tf_op jit(solution)/shard_map/ppermute | solution.py:254
  198.1 4.3 %all-to-all-done.1 = bf16[256,7,2,128]{3,2,1,0:T(2,128)(2,1)} async-done(((bf16[256,7,2,128]{3,2,1,0:T(2,128)(2,1)}), bf16[256,7,2,128]{3,2,1,0:T(2,128)(2,1)}, u32[]{:S(2)}, u32[]{:S(2)}) %all-to-all-start.1) | async-done | bytes 917536 | tf_op jit(solution)/shard_map/all_to_all | solution.py:247
  202.4 1.4 copy.69
  203.8 4.1 %shard_map.48 = bf16[4,112,896]{2,1,0:T(8,128)(2,1)S(1)} custom-call(bf16[7,2,4,64,128]{4,3,2,1,0:T(8,128)(2,1)S(1)} %bitcast.159, bf16[3,896,1024]{2,1,0:T(8,128)(2,1)} %maximum_maximum_fusion.loop_ref), custom_call_target="tpu_custom_call" | custom-call | tf_op jit(solution)/shard_map/pallas_call | solution.py:190
  207.9 2.2 collective-permute-done.3
  210.1 9.9 %collective-permute-done.4 = bf16[112,896]{1,0:T(8,128)(2,1)S(1)} collective-permute-done((bf16[112,896]{1,0:T(8,128)(2,1)}, bf16[112,896]{1,0:T(8,128)(2,1)S(1)}, u32[]{:S(2)}, u32[]{:S(2)}) %collective-permute-start.4) | collective-permute-done | bytes 200736 | tf_op jit(solution)/shard_map/ppermute | solution.py:254
  220.1 23.0 %collective-permute-start = (bf16[112,896]{1,0:T(8,128)(2,1)S(1)}, bf16[112,896]{1,0:T(8,128)(2,1)S(1)}, u32[]{:S(2)}, u32[]{:S(2)}) collective-permute-start(bf16[112,896]{1,0:T(8,128)(2,1)S(1)} %get-tuple-element.32), channel_id=1, source_target_pairs={{0,3},{1,2},{2,1},{3,0},{4,7},{5,6},{6,5},{7,4},{8,11},{9,10},{10,... | collective-permute-start | bytes 602120 | tf_op jit(solution)/shard_map/ppermute | solution.py:254
  243.1 0.7 copy-done.8
  243.8 1.4 select_bitcast_fusion.7
  245.2 0.4 collective-permute-start.2
  245.6 1.0 select_bitcast_fusion.3
  246.7 9.5 %collective-permute-done = bf16[112,896]{1,0:T(8,128)(2,1)S(1)} collective-permute-done((bf16[112,896]{1,0:T(8,128)(2,1)S(1)}, bf16[112,896]{1,0:T(8,128)(2,1)S(1)}, u32[]{:S(2)}, u32[]{:S(2)}) %collective-permute-start) | collective-permute-done | bytes 200736 | tf_op jit(solution)/shard_map/ppermute | solution.py:254
  256.1 4.3 %collective-permute-done.1 = bf16[112,896]{1,0:T(8,128)(2,1)S(1)} collective-permute-done((bf16[112,896]{1,0:T(8,128)(2,1)S(1)}, bf16[112,896]{1,0:T(8,128)(2,1)S(1)}, u32[]{:S(2)}, u32[]{:S(2)}) %collective-permute-start.1) | collective-permute-done | bytes 200736 | tf_op jit(solution)/shard_map/ppermute | solution.py:254
  260.6 0.7 add_convert_fusion.2
  261.3 1.7 pad_maximum_fusion
  (62 shorter events, 1.4 us)
Async XLA Ops:
  3.5 1.6 copy-start
  5.2 11.3 %copy-start.11 = (s32[7,3]{0,1:T(4,128)S(1)}, s32[7,3]{0,1:T(4,128)}, u32[]{:S(2)}) copy-start(s32[7,3]{0,1:T(4,128)} %param.7) | copy-start | bytes 256
  5.2 12.1 %copy-start.10 = (f32[6,256]{1,0:T(8,128)S(1)}, f32[6,256]{1,0:T(8,128)}, u32[]{:S(2)}) copy-start(f32[6,256]{1,0:T(8,128)} %param.6) | copy-start | bytes 18436
  5.2 75.5 %all-to-all-start = ((bf16[64,21,8,128]{3,2,1,0:T(8,128)(2,1)}), bf16[64,21,8,128]{3,2,1,0:T(8,128)(2,1)S(1)}, u32[]{:S(2)}, u32[]{:S(2)}) async-start(bf16[64,21,8,128]{3,2,1,0:T(8,128)(2,1)} %copy-done), calls=%async_computation | async-start | bytes 5505024 | tf_op jit(solution)/shard_map/all_to_all | solution.py:217
  43.9 4.8 %copy-start.9 = (f32[42,256]{1,0:T(8,128)S(1)}, f32[42,256]{1,0:T(8,128)}, u32[]{:S(2)}) copy-start(f32[42,256]{1,0:T(8,128)} %reshape.921) | copy-start | bytes 129028
  49.3 1.8 copy-start.4
  80.7 1.0 copy-start.1
  90.5 38.9 %all-to-all-start.2 = ((bf16[256,7,2,128]{3,2,1,0:T(2,128)(2,1)}), bf16[256,7,2,128]{3,2,1,0:T(2,128)(2,1)}, u32[]{:S(2)}, u32[]{:S(2)}) async-start(bf16[256,7,2,128]{3,2,1,0:T(2,128)(2,1)} %bitcast.166), calls=%async_computation.2 | async-start | bytes 1835008 | tf_op jit(solution)/shard_map/all_to_all | solution.py:247
  101.5 1.0 copy-start.2
  129.5 36.2 %all-to-all-start.3 = ((bf16[256,7,2,128]{3,2,1,0:T(2,128)(2,1)}), bf16[256,7,2,128]{3,2,1,0:T(2,128)(2,1)}, u32[]{:S(2)}, u32[]{:S(2)}) async-start(bf16[256,7,2,128]{3,2,1,0:T(2,128)(2,1)} %bitcast.165), calls=%async_computation.3 | async-start | bytes 1835008 | tf_op jit(solution)/shard_map/all_to_all | solution.py:247
  137.8 1.0 copy-start.3
  165.7 36.7 %all-to-all-start.1 = ((bf16[256,7,2,128]{3,2,1,0:T(2,128)(2,1)}), bf16[256,7,2,128]{3,2,1,0:T(2,128)(2,1)}, u32[]{:S(2)}, u32[]{:S(2)}) async-start(bf16[256,7,2,128]{3,2,1,0:T(2,128)(2,1)} %bitcast.149), calls=%async_computation.1 | async-start | bytes 1835008 | tf_op jit(solution)/shard_map/all_to_all | solution.py:247
  180.4 29.7 %collective-permute-start.3 = (bf16[112,896]{1,0:T(8,128)(2,1)}, bf16[112,896]{1,0:T(8,128)(2,1)S(1)}, u32[]{:S(2)}, u32[]{:S(2)}) collective-permute-start(bf16[112,896]{1,0:T(8,128)(2,1)} %get-tuple-element.35), channel_id=1, source_target_pairs={{0,3},{1,2},{2,1},{3,0},{4,7},{5,6},{6,5},{7,4},{8,11},{9,10},{10,... | collective-permute-start | bytes 602120 | tf_op jit(solution)/shard_map/ppermute | solution.py:254
  185.9 34.2 %collective-permute-start.4 = (bf16[112,896]{1,0:T(8,128)(2,1)}, bf16[112,896]{1,0:T(8,128)(2,1)S(1)}, u32[]{:S(2)}, u32[]{:S(2)}) collective-permute-start(bf16[112,896]{1,0:T(8,128)(2,1)} %get-tuple-element.34), channel_id=1, source_target_pairs={{0,2},{1,3},{2,0},{3,1},{4,6},{5,7},{6,4},{7,5},{8,10},{9,11},{10,... | collective-permute-start | bytes 602120 | tf_op jit(solution)/shard_map/ppermute | solution.py:254
  186.0 57.0 %collective-permute-start.5 = (bf16[112,896]{1,0:T(8,128)(2,1)}, bf16[112,896]{1,0:T(8,128)(2,1)S(1)}, u32[]{:S(2)}, u32[]{:S(2)}) collective-permute-start(bf16[112,896]{1,0:T(8,128)(2,1)} %get-tuple-element.33), channel_id=1, source_target_pairs={{0,1},{1,0},{2,3},{3,2},{4,5},{5,4},{6,7},{7,6},{8,9},{9,8},{10,11... | collective-permute-start | bytes 602120 | tf_op jit(solution)/shard_map/ppermute | solution.py:254
  192.8 52.4 %collective-permute-start.6 = (bf16[112,896]{1,0:T(8,128)(2,1)}, bf16[112,896]{1,0:T(8,128)(2,1)S(1)}, u32[]{:S(2)}, u32[]{:S(2)}) collective-permute-start(bf16[112,896]{1,0:T(8,128)(2,1)} %get-tuple-element.38), channel_id=1, source_target_pairs={{0,3},{1,2},{2,1},{3,0},{4,7},{5,6},{6,5},{7,4},{8,11},{9,10},{10,... | collective-permute-start | bytes 602120 | tf_op jit(solution)/shard_map/ppermute | solution.py:254
  198.0 47.6 %collective-permute-start.7 = (bf16[112,896]{1,0:T(8,128)(2,1)}, bf16[112,896]{1,0:T(8,128)(2,1)}, u32[]{:S(2)}, u32[]{:S(2)}) collective-permute-start(bf16[112,896]{1,0:T(8,128)(2,1)} %get-tuple-element.37), channel_id=1, source_target_pairs={{0,2},{1,3},{2,0},{3,1},{4,6},{5,7},{6,4},{7,5},{8,10},{9,11},{10,... | collective-permute-start | bytes 602120 | tf_op jit(solution)/shard_map/ppermute | solution.py:254
  210.1 32.9 %copy-start.6 = (bf16[112,896]{1,0:T(8,128)(2,1)}, bf16[112,896]{1,0:T(8,128)(2,1)S(1)}, u32[]{:S(2)}) copy-start(bf16[112,896]{1,0:T(8,128)(2,1)S(1)} %collective-permute-done.3) | copy-start | bytes 602116
  210.1 35.5 %collective-permute-start.8 = (bf16[112,896]{1,0:T(8,128)(2,1)}, bf16[112,896]{1,0:T(8,128)(2,1)S(1)}, u32[]{:S(2)}, u32[]{:S(2)}) collective-permute-start(bf16[112,896]{1,0:T(8,128)(2,1)} %get-tuple-element.36), channel_id=1, source_target_pairs={{0,1},{1,0},{2,3},{3,2},{4,5},{5,4},{6,7},{7,6},{8,9},{9,8},{10,11... | collective-permute-start | bytes 602120 | tf_op jit(solution)/shard_map/ppermute | solution.py:254
  220.1 23.0 %copy-start.7 = (bf16[112,896]{1,0:T(8,128)(2,1)}, bf16[112,896]{1,0:T(8,128)(2,1)S(1)}, u32[]{:S(2)}) copy-start(bf16[112,896]{1,0:T(8,128)(2,1)S(1)} %collective-permute-done.4) | copy-start | bytes 602116
  220.1 36.1 %collective-permute-start = (bf16[112,896]{1,0:T(8,128)(2,1)S(1)}, bf16[112,896]{1,0:T(8,128)(2,1)S(1)}, u32[]{:S(2)}, u32[]{:S(2)}) collective-permute-start(bf16[112,896]{1,0:T(8,128)(2,1)S(1)} %get-tuple-element.32), channel_id=1, source_target_pairs={{0,3},{1,2},{2,1},{3,0},{4,7},{5,6},{6,5},{7,4},{8,11},{9,10},{10,... | collective-permute-start | bytes 602120 | tf_op jit(solution)/shard_map/ppermute | solution.py:254
  243.0 0.7 copy-start.8
  243.7 16.8 %copy-start.5 = (bf16[3,4,112,896]{3,2,1,0:T(8,128)(2,1)S(1)}, bf16[3,4,112,896]{3,2,1,0:T(8,128)(2,1)}, u32[]{:S(2)}) copy-start(bf16[3,4,112,896]{3,2,1,0:T(8,128)(2,1)} %v_ref.1) | copy-start | bytes 7225348
  243.7 16.7 %collective-permute-start.1 = (bf16[112,896]{1,0:T(8,128)(2,1)S(1)}, bf16[112,896]{1,0:T(8,128)(2,1)S(1)}, u32[]{:S(2)}, u32[]{:S(2)}) collective-permute-start(bf16[112,896]{1,0:T(8,128)(2,1)S(1)} %get-tuple-element.31), channel_id=1, source_target_pairs={{0,2},{1,3},{2,0},{3,1},{4,6},{5,7},{6,4},{7,5},{8,10},{9,11},{10,... | collective-permute-start | bytes 602120 | tf_op jit(solution)/shard_map/ppermute | solution.py:254
  245.2 15.3 %collective-permute-start.2 = (bf16[112,896]{1,0:T(8,128)(2,1)S(1)}, bf16[112,896]{1,0:T(8,128)(2,1)S(1)}, u32[]{:S(2)}, u32[]{:S(2)}) collective-permute-start(bf16[112,896]{1,0:T(8,128)(2,1)S(1)} %get-tuple-element.30), channel_id=1, source_target_pairs={{0,1},{1,0},{2,3},{3,2},{4,5},{5,4},{6,7},{7,6},{8,9},{9,8},{10,11... | collective-permute-start | bytes 602120 | tf_op jit(solution)/shard_map/ppermute | solution.py:254
